TPU v7x, 256 devices: a whole 4x4x8 slice. The times are simulated.
256 devices in a mesh: sub: 32 (over z, y), grp: 8 (over x, core).
Axes of the slice: x: 4, y: 4, z: 8, core: 2. Of those that a mesh axis runs over, the one named last changes fastest.
Arguments:
- multipliers: float32 [1024, 32, 512], P(('sub', 'grp')), may hold values from -6 to 6
- residual: float32 [1024, 32, 512], P(('sub', 'grp')), may hold values from -40 to 40
- old_direction: float32 [1024, 32, 512], P(('sub', 'grp')), may hold values from -6 to 6
- old_norms: float32 [32], replicated, may hold values from 524288 to 4194304
- matching: int32 [1024, 512], P(('sub', 'grp')), may hold values from 0 to 511, each once within a row
- factor_inverse: bfloat16 [1024, 1024, 1024], P(('sub', 'grp')), may hold values from -1 to 1.5, as said below
- rigid_modes: float32 [1024, 6, 1024], P(('sub', 'grp')), may hold values from -0.4375 to 0.4375
- coarse_inverse: float32 [6144, 6144], P(('sub', 'grp')), may hold values from -1 to 1.6, as said below
Outputs:
- new_multipliers: float32 [1024, 32, 512], P(('sub', 'grp'))
- new_residual: float32 [1024, 32, 512], P(('sub', 'grp'))
- direction: float32 [1024, 32, 512], P(('sub', 'grp'))
Inputs may be any that keep to these rules, and one draw needn't show every extreme that they name: `matching`: each row is a permutation of 0 to 511. `factor_inverse`: lower triangular with a positive diagonal. `coarse_inverse`: symmetric.
All inputs are finite; a program needn't handle non-finite values.
Results may differ from a plain program's by a relative error of at most 0.0021.
Values sent between devices are 32-bit elements; how exact they have to be, the bound alone decides.
A program may use at most 64 MiB of HBM per device.

v0:
```python
import jax
import jax.numpy as jnp
from jax import lax
from jax.sharding import Mesh
from jax.sharding import PartitionSpec as P

SUB_GRP = ("sub_0", "sub_1", "grp_0", "grp_1")


def shifted(block, axis, distance):
    devices = range(lax.axis_size(axis))
    route = [(i - distance, i) for i in devices if i - distance in devices]
    return lax.ppermute(block, axis, route)


def sent_to_all(shard, axis):
    copies = jnp.broadcast_to(shard, (lax.axis_size(axis), *shard.shape))
    return lax.all_to_all(copies, axis, split_axis=0, concat_axis=0, tiled=True)


def of_everyone(shard, axis):
    everything = sent_to_all(shard, axis)
    return jnp.sum(everything, axis=0)


def by_axis(shard, axes):
    far, near = axes
    nearer = of_everyone(shard, near)
    return of_everyone(nearer, far)


def joined_along(blocks, dim):
    blocks = jnp.moveaxis(blocks, 0, dim)
    dims = blocks.shape
    return blocks.reshape(*dims[:dim], dims[dim] * dims[dim + 1], *dims[dim + 2 :])


def gathered_by_axis(shard, axes, dim):
    far, near = axes
    leading = sent_to_all(shard, far)
    blocks = jnp.swapaxes(sent_to_all(leading, near), 0, 1)
    return joined_along(blocks.reshape(-1, *shard.shape), dim)


def before_faces(values):
    incoming = shifted(values[values.shape[0] - 1 :], SUB_GRP, 1)
    return jnp.concatenate([incoming, values[:-1]], 0)


def interface(values, match_table, retain):
    before = before_faces(values)
    leftward = -jnp.einsum("sck,sjk->scj", before, match_table, precision=lax.Precision.HIGHEST)
    return jnp.concatenate([leftward, values * retain[:, None, None]], 2)


def assemble(local_sol, match_table, retain):
    middle = local_sol.shape[2] // 2
    leftpart = local_sol[:, :, :middle]
    returned = jnp.einsum("sci,sik->sck", leftpart, match_table, precision=lax.Precision.HIGHEST)
    incoming = shifted(returned[:1], SUB_GRP, -1)
    following = jnp.concatenate([returned[1:], incoming], 0)
    return (local_sol[:, :, middle:] - following) * retain[:, None, None]


def inner_sums(first_field, second_field):
    return by_axis(
        jnp.sum(first_field * second_field, axis=(0, 2)), (("sub_0", "sub_1"), ("grp_0", "grp_1"))
    )


def on_device(
    multipliers,
    residual,
    old_direction,
    old_norms,
    matching,
    factor_inverse,
    rigid_modes,
    coarse_inverse,
):
    count = multipliers.shape[0]
    cases = multipliers.shape[1]
    ranks = rigid_modes.shape[1]
    half_width = matching.shape[1]
    own_rows = count * ranks
    global_ids = lax.axis_index(SUB_GRP) * count + jnp.arange(count, dtype=jnp.int32)
    total_subs = count * lax.axis_size(SUB_GRP)
    retain = (global_ids != total_subs - 1).astype(jnp.float32)
    positions = lax.broadcasted_iota(jnp.int32, (1, 1, half_width), 2)
    match_table = (matching[:, :, None] == positions).astype(jnp.float32)
    masked = residual * retain[:, None, None]
    xres = interface(masked, match_table, retain)
    modes = jnp.einsum("smj,scj->smc", rigid_modes, xres, precision=lax.Precision.HIGHEST)
    modes = modes.reshape(own_rows, cases)
    coeffs = jnp.dot(
        coarse_inverse,
        gathered_by_axis(modes, (("sub_0", "sub_1"), ("grp_0", "grp_1")), 0),
        precision=lax.Precision.HIGHEST,
    )
    coeffs = coeffs.reshape(count, ranks, cases)
    spread = jnp.einsum("smj,smc->scj", rigid_modes, coeffs, precision=lax.Precision.HIGHEST)
    projected = masked - assemble(spread, match_table, retain)
    norms = inner_sums(projected, projected)
    direction = (
        projected + (norms / old_norms)[None, :, None] * old_direction * retain[:, None, None]
    )
    xdir = interface(direction, match_table, retain).astype(jnp.bfloat16)
    inner = jnp.einsum(
        "scj,sij->sci", xdir, factor_inverse, preferred_element_type=jnp.float32
    ).astype(jnp.bfloat16)
    solved = jnp.einsum("sci,sij->scj", inner, factor_inverse, preferred_element_type=jnp.float32)
    image = assemble(solved, match_table, retain)
    curvature = inner_sums(direction, image)
    step_len = (norms / curvature)[None, :, None]
    return (multipliers + step_len * direction, masked - step_len * image, direction)


def solution(mesh):
    torus = Mesh(mesh.devices.reshape(8, 4, 4, 2), ("sub_0", "sub_1", "grp_0", "grp_1"))
    placed = (
        P(SUB_GRP, None, None),
        P(SUB_GRP, None, None),
        P(SUB_GRP, None, None),
        P(),
        P(SUB_GRP, None),
        P(SUB_GRP, None, None),
        P(SUB_GRP, None, None),
        P(SUB_GRP, None),
    )
    return jax.shard_map(
        on_device,
        mesh=torus,
        in_specs=placed,
        out_specs=(P(SUB_GRP, None, None), P(SUB_GRP, None, None), P(SUB_GRP, None, None)),
        check_vma=False,
    )
```

profile of v0, /device:TPU:1, one launch (start us, length us, event | category | flops | bytes accessed | tf_op | source)
XLA Modules:
  0.0 159.9 jit_solution(13464186053439893950)
XLA Ops:
  0.6 0.0 copy-start
  0.7 1.1 broadcast_multiply_fusion
  1.8 4.5 %collective-permute-start = (f32[1,32,512]{2,1,0:T(8,128)S(1)}, f32[1,32,512]{2,1,0:T(8,128)S(1)}, u32[]{:S(2)}, u32[]{:S(2)}) collective-permute-start(f32[1,32,512]{2,1,0:T(8,128)S(1)} %slice.48), channel_id=1, source_target_pairs={{0,1},{1,2},{2,3},{3,4},{4,5},{5,6},{6,7},{7,8},{8,9},{9,10},{10,1... | collective-permute-start | bytes 196616 | tf_op jit(solution)/shard_map/ppermute | solution.py:13
  6.3 1.3 collective-permute-done
  7.6 2.8 %fusion.8 = f32[4,32,512]{2,1,0:T(8,128)S(1)} fusion(s32[4,512]{1,0:T(4,128)} %param.12, f32[3,32,512]{2,1,0:T(8,128)S(1)} %slice.49, f32[1,32,512]{2,1,0:T(8,128)S(1)} %collective-permute-done), kind=kOutput, calls=%fused_computation.10 | convolution fusion | flops 403832832 | bytes 532480 | tf_op jit(solution)/shard_map/sck,sjk->scj/dot_general | solution.py:52
  10.5 1.5 convolution_bitcast_fusion
  12.0 0.2 reshape.43
  12.2 20.1 %all_to_all.34 = f32[32,1,768]{2,1,0:T(1,128)S(1)} all-to-all(f32[32,1,768]{2,1,0:T(1,128)S(1)} %reshape.43), channel_id=1, replica_groups=mesh['sub_0'=8,'sub_1'=4,'grp_0'=4,'grp_1'=2] {'sub_0','sub_1'}, dimensions={0} | all-to-all | bytes 196608 | tf_op jit(solution)/shard_map/all_to_all | solution.py:18
  32.3 0.5 broadcast.27
  32.8 0.9 reduce.4
  33.7 0.1 reshape.44
  33.8 1.9 %broadcast_in_dim.13 = f32[8,32,24,32]{3,2,1,0:T(8,128)} broadcast(f32[32,24,32]{2,1,0:T(8,128)S(1)} %reshape.44), dimensions={1,2,3} | broadcast | bytes 884736 | tf_op jit(solution)/shard_map/broadcast_in_dim | solution.py:17
  35.7 2.8 %reshape.45 = f32[8,1,24576]{2,1,0:T(1,128)S(1)} reshape(f32[8,32,24,32]{3,2,1,0:T(8,128)} %broadcast_in_dim.13) | data formatting | bytes 1572864
  38.5 20.0 %all_to_all.35 = f32[8,1,24576]{2,1,0:T(1,128)S(1)} all-to-all(f32[8,1,24576]{2,1,0:T(1,128)S(1)} %reshape.45), channel_id=1, replica_groups=mesh['sub_0'=8,'sub_1'=4,'grp_0'=4,'grp_1'=2] {'grp_0','grp_1'}, dimensions={0} | all-to-all | bytes 1572864 | tf_op jit(solution)/shard_map/all_to_all | solution.py:18
  58.6 2.5 %reduce.5 = f32[8,24576]{1,0:T(8,128)S(1)} reduce(f32[8,1,24576]{2,1,0:T(1,128)S(1)} %all_to_all.35, f32[]{:T(128)} %broadcast.27), dimensions={1}, to_apply=%all_to_all.23.reduce_sub_computation | reduce | bytes 1572868 | tf_op jit(solution)/shard_map/all_to_all | solution.py:18
  61.1 2.7 %reshape.46 = f32[8,32,24,32]{3,2,1,0:T(8,128)} reshape(f32[8,24576]{1,0:T(8,128)S(1)} %reduce.5) | data formatting | bytes 1572864
  63.8 5.2 %copy.23 = f32[32,8,24,32]{2,1,0,3:T(8,128)} copy(f32[32,8,24,32]{3,2,0,1:T(8,128)} %bitcast.18) | data formatting | bytes 1572864 | tf_op jit(solution)/shard_map/transpose | solution.py:41
  69.0 0.0 copy-start.2
  69.0 4.2 %reshape_reshape.3 = f32[6144,32]{0,1:T(8,128)S(1)} reshape(f32[32,8,24,32]{2,1,0,3:T(8,128)} %copy.23) | data formatting | bytes 1572864 | tf_op jit(solution)/shard_map/reshape;reshape | solution.py:35
  73.2 0.0 copy-done
  73.2 0.7 convolution_bitcast_fusion.1
  73.9 0.0 copy-done.2
  73.9 0.6 fusion.32
  74.6 0.0 copy-done.5
  74.6 1.8 %fusion.2 = f32[4,32,512]{2,1,0:T(8,128)S(1)} fusion(s32[4,512]{1,0:T(4,128)S(1)} %copy-done.5, f32[4,32,1024]{2,1,0:T(8,128)S(1)} %fusion.32), kind=kOutput, calls=%fused_computation.3 | convolution fusion | flops 403701760 | bytes 532480 | tf_op jit(solution)/shard_map/sci,sik->sck/dot_general | solution.py:59
  76.4 3.0 %collective-permute-start.1 = (f32[1,32,512]{2,1,0:T(8,128)S(1)}, f32[1,32,512]{2,1,0:T(8,128)S(1)}, u32[]{:S(2)}, u32[]{:S(2)}) collective-permute-start(f32[1,32,512]{2,1,0:T(8,128)S(1)} %slice.53), channel_id=1, source_target_pairs={{1,0},{2,1},{3,2},{4,3},{5,4},{6,5},{7,6},{8,7},{9,8},{10,9},{11,1... | collective-permute-start | bytes 196616 | tf_op jit(solution)/shard_map/ppermute | solution.py:13
  79.4 2.6 %collective-permute-done.1 = f32[1,32,512]{2,1,0:T(8,128)S(1)} collective-permute-done((f32[1,32,512]{2,1,0:T(8,128)S(1)}, f32[1,32,512]{2,1,0:T(8,128)S(1)}, u32[]{:S(2)}, u32[]{:S(2)}) %collective-permute-start.1) | collective-permute-done | bytes 65568 | tf_op jit(solution)/shard_map/ppermute | solution.py:13
  82.0 0.2 multiply_reduce_fusion.1
  82.3 9.1 %all_to_all.36 = f32[8,1,32]{2,1,0:T(1,128)S(1)} all-to-all(f32[8,1,32]{2,1,0:T(1,128)S(1)} %broadcast_in_dim.14), channel_id=1, replica_groups=mesh['sub_0'=8,'sub_1'=4,'grp_0'=4,'grp_1'=2] {'grp_0','grp_1'}, dimensions={0} | all-to-all | bytes 2048 | tf_op jit(solution)/shard_map/all_to_all | solution.py:18
  91.3 14.8 %all_to_all.37 = f32[32,1,32]{2,1,0:T(1,128)S(1)} all-to-all(f32[32,1,32]{2,1,0:T(1,128)S(1)} %broadcast_in_dim.30), channel_id=1, replica_groups=mesh['sub_0'=8,'sub_1'=4,'grp_0'=4,'grp_1'=2] {'sub_0','sub_1'}, dimensions={0} | all-to-all | bytes 8192 | tf_op jit(solution)/shard_map/all_to_all | solution.py:18
  106.2 0.0 copy-done.6
  106.2 0.0 copy-done.4
  106.2 0.1 multiply_convert_fusion
  106.3 0.0 copy-start.1
  106.3 4.4 %collective-permute-start.2 = (f32[1,32,512]{2,1,0:T(8,128)S(1)}, f32[1,32,512]{2,1,0:T(8,128)S(1)}, u32[]{:S(2)}, u32[]{:S(2)}) collective-permute-start(f32[1,32,512]{2,1,0:T(8,128)S(1)} %slice.54), channel_id=1, source_target_pairs={{0,1},{1,2},{2,3},{3,4},{4,5},{5,6},{6,7},{7,8},{8,9},{9,10},{10,1... | collective-permute-start | bytes 196616 | tf_op jit(solution)/shard_map/ppermute | solution.py:13
  110.8 1.1 collective-permute-done.2
  111.9 2.4 %fusion.10 = bf16[4,32,512]{2,1,0:T(8,128)(2,1)S(1)} fusion(s32[4,512]{1,0:T(4,128)S(1)} %copy-done.5, f32[3,32,512]{2,1,0:T(8,128)S(1)} %slice.55, f32[1,32,512]{2,1,0:T(8,128)S(1)} %collective-permute-done.2), kind=kOutput, calls=%fused_computation.12 | convolution fusion | flops 403898368 | bytes 401408 | tf_op jit(solution)/shard_map/sck,sjk->scj/dot_general | solution.py:52
  114.2 0.0 copy-start.3
  114.3 9.8 %fusion.11 = f32[4,32,1024]{2,1,0:T(8,128)S(1)} fusion(bf16[4,1024,1024]{2,1,0:T(8,128)(2,1)} %param.13, bf16[4,32,512]{2,1,0:T(8,128)(2,1)S(1)} %get-tuple-element.3, bf16[4,32,512]{2,1,0:T(8,128)(2,1)S(1)} %fusion.10), kind=kOutput, calls=%fused_computation.15 | convolution fusion | flops 537526272 | bytes 9175040 | tf_op jit(solution)/shard_map/sci,sij->scj/dot_general | solution.py:111
  124.1 1.8 %fusion = f32[4,32,512]{2,1,0:T(8,128)S(1)} fusion(s32[4,512]{1,0:T(4,128)S(1)} %copy-done.5, f32[4,32,1024]{2,1,0:T(8,128)S(1)} %fusion.11), kind=kOutput, calls=%fused_computation.1 | convolution fusion | flops 403701760 | bytes 532480 | tf_op jit(solution)/shard_map/sci,sik->sck/dot_general | solution.py:59
  125.9 1.9 %collective-permute-start.3 = (f32[1,32,512]{2,1,0:T(8,128)S(1)}, f32[1,32,512]{2,1,0:T(8,128)S(1)}, u32[]{:S(2)}, u32[]{:S(2)}) collective-permute-start(f32[1,32,512]{2,1,0:T(8,128)S(1)} %slice.59), channel_id=1, source_target_pairs={{1,0},{2,1},{3,2},{4,3},{5,4},{6,5},{7,6},{8,7},{9,8},{10,9},{11,1... | collective-permute-start | bytes 196616 | tf_op jit(solution)/shard_map/ppermute | solution.py:13
  127.9 4.3 %collective-permute-done.3 = f32[1,32,512]{2,1,0:T(8,128)S(1)} collective-permute-done((f32[1,32,512]{2,1,0:T(8,128)S(1)}, f32[1,32,512]{2,1,0:T(8,128)S(1)}, u32[]{:S(2)}, u32[]{:S(2)}) %collective-permute-start.3) | collective-permute-done | bytes 65568 | tf_op jit(solution)/shard_map/ppermute | solution.py:13
  132.1 0.2 multiply_reduce_fusion
  132.3 10.6 %all_to_all.38 = f32[8,1,32]{2,1,0:T(1,128)S(1)} all-to-all(f32[8,1,32]{2,1,0:T(1,128)S(1)} %broadcast_in_dim.31), channel_id=1, replica_groups=mesh['sub_0'=8,'sub_1'=4,'grp_0'=4,'grp_1'=2] {'grp_0','grp_1'}, dimensions={0} | all-to-all | bytes 2048 | tf_op jit(solution)/shard_map/all_to_all | solution.py:18
  143.0 15.9 %all_to_all.39 = f32[32,1,32]{2,1,0:T(1,128)S(1)} all-to-all(f32[32,1,32]{2,1,0:T(1,128)S(1)} %broadcast_in_dim.32), channel_id=1, replica_groups=mesh['sub_0'=8,'sub_1'=4,'grp_0'=4,'grp_1'=2] {'sub_0','sub_1'}, dimensions={0} | all-to-all | bytes 8192 | tf_op jit(solution)/shard_map/all_to_all | solution.py:18
  158.9 0.0 copy-done.1
  158.9 0.0 copy-done.3
  158.9 1.0 multiply_subtract_fusion
  (25 shorter events, 0.3 us)
Async XLA Ops:
  0.6 72.5 %copy-start = (f32[24,6144]{1,0:T(8,128)S(1)}, f32[24,6144]{1,0:T(8,128)}, u32[]{:S(2)}) copy-start(f32[24,6144]{1,0:T(8,128)} %param.15) | copy-start | bytes 1769476
  1.8 5.8 %collective-permute-start = (f32[1,32,512]{2,1,0:T(8,128)S(1)}, f32[1,32,512]{2,1,0:T(8,128)S(1)}, u32[]{:S(2)}, u32[]{:S(2)}) collective-permute-start(f32[1,32,512]{2,1,0:T(8,128)S(1)} %slice.48), channel_id=1, source_target_pairs={{0,1},{1,2},{2,3},{3,4},{4,5},{5,6},{6,7},{7,8},{8,9},{9,10},{10,1... | collective-permute-start | bytes 196616 | tf_op jit(solution)/shard_map/ppermute | solution.py:13
  69.0 4.9 %copy-start.2 = (f32[4,6,1024]{2,0,1:T(4,128)S(1)}, f32[4,6,1024]{2,0,1:T(4,128)}, u32[]{:S(2)}) copy-start(f32[4,6,1024]{2,0,1:T(4,128)} %param.14) | copy-start | bytes 294916
  69.0 5.6 %copy-start.5 = (s32[4,512]{1,0:T(4,128)S(1)}, s32[4,512]{1,0:T(4,128)}, u32[]{:S(2)}) copy-start(s32[4,512]{1,0:T(4,128)} %param.12) | copy-start | bytes 24580
  69.0 37.2 %copy-start.6 = (f32[32]{0:T(128)S(1)}, f32[32]{0:T(128)}, u32[]{:S(2)}) copy-start(f32[32]{0:T(128)} %param.11) | copy-start | bytes 388
  69.0 37.2 %copy-start.4 = (f32[4,32,512]{2,1,0:T(8,128)S(1)}, f32[4,32,512]{2,1,0:T(8,128)}, u32[]{:S(2)}) copy-start(f32[4,32,512]{2,1,0:T(8,128)} %param.10) | copy-start | bytes 786436
  76.4 5.6 %collective-permute-start.1 = (f32[1,32,512]{2,1,0:T(8,128)S(1)}, f32[1,32,512]{2,1,0:T(8,128)S(1)}, u32[]{:S(2)}, u32[]{:S(2)}) collective-permute-start(f32[1,32,512]{2,1,0:T(8,128)S(1)} %slice.53), channel_id=1, source_target_pairs={{1,0},{2,1},{3,2},{4,3},{5,4},{6,5},{7,6},{8,7},{9,8},{10,9},{11,1... | collective-permute-start | bytes 196616 | tf_op jit(solution)/shard_map/ppermute | solution.py:13
  106.3 52.6 %copy-start.1 = (f32[4,32,512]{2,1,0:T(8,128)}, f32[4,32,512]{2,1,0:T(8,128)S(1)}, u32[]{:S(2)}) copy-start(f32[4,32,512]{2,1,0:T(8,128)S(1)} %get-tuple-element.4) | copy-start | bytes 786436
  106.3 5.5 %collective-permute-start.2 = (f32[1,32,512]{2,1,0:T(8,128)S(1)}, f32[1,32,512]{2,1,0:T(8,128)S(1)}, u32[]{:S(2)}, u32[]{:S(2)}) collective-permute-start(f32[1,32,512]{2,1,0:T(8,128)S(1)} %slice.54), channel_id=1, source_target_pairs={{0,1},{1,2},{2,3},{3,4},{4,5},{5,6},{6,7},{7,8},{8,9},{9,10},{10,1... | collective-permute-start | bytes 196616 | tf_op jit(solution)/shard_map/ppermute | solution.py:13
  114.2 44.7 %copy-start.3 = (f32[4,32,512]{2,1,0:T(8,128)S(1)}, f32[4,32,512]{2,1,0:T(8,128)}, u32[]{:S(2)}) copy-start(f32[4,32,512]{2,1,0:T(8,128)} %param.8) | copy-start | bytes 786436
  125.9 6.2 %collective-permute-start.3 = (f32[1,32,512]{2,1,0:T(8,128)S(1)}, f32[1,32,512]{2,1,0:T(8,128)S(1)}, u32[]{:S(2)}, u32[]{:S(2)}) collective-permute-start(f32[1,32,512]{2,1,0:T(8,128)S(1)} %slice.59), channel_id=1, source_target_pairs={{1,0},{2,1},{3,2},{4,3},{5,4},{6,5},{7,6},{8,7},{9,8},{10,9},{11,1... | collective-permute-start | bytes 196616 | tf_op jit(solution)/shard_map/ppermute | solution.py:13
where the time goes:
time: 160 us
  blocking collectives  90.5 us (57%)
  matrix products  21.5 us (13%)
  local copies, waits for them, and re-layouts  17.8 us (11%)
  starting transfers between devices  13.8 us (9%)
  waiting for transfers between devices  9.25 us (6%)
  other arithmetic  6.11 us (4%)
    all_to_all x6, blocking collectives, sent_to_all(): return lax.all_to_all(copies, axis, split_axis=0, concat_axis=0, tiled=True)  90.5 us
    ppermute x4, starting transfers between devices, shifted(): return lax.ppermute(block, axis, route)  13.8 us
    dot_general x1, matrix products, on_device(): jnp.einsum('sci,sij->scj', inner, factor_inverse, preferred_element_type=...  9.82 us
    ppermute x4, waiting for transfers between devices, shifted(): return lax.ppermute(block, axis, route)  9.25 us
    unnamed x18, local copies, waits for them, and re-layouts  5.9 us
    dot_general x2, matrix products, interface(): jnp.einsum('sck,sjk->scj', before, match_table, precision=lax.Precision.H...  5.22 us
    transpose x1, local copies, waits for them, and re-layouts, gathered_by_axis(): blocks = jnp.swapaxes(sent_to_all(leading, near), 0, 1)  5.2 us
    another operation x1, local copies, waits for them, and re-layouts, joined_along(): blocks.reshape(*dims[:dim], dims[dim] * dims[dim + 1], *dims[dim + 2:])  4.15 us
  transfers between devices with their start and end apart: 4, of which 4 were waited for; matrix products, arithmetic and copies ran while one was open for 0% of the time, Pallas kernels for 0%

commit v1 on v0

v1 whole, which is shorter than its diff:
```python
import functools

import jax
import jax.numpy as jnp
from jax import lax
from jax.experimental import pallas as pl
from jax.experimental.pallas import tpu as pltpu
from jax.sharding import PartitionSpec as P

F32 = jnp.float32
BF16 = jnp.bfloat16
HIGHEST = lax.Precision.HIGHEST
CHUNKS = 4
LANES = 128
NN = (((1,), (0,)), ((), ()))
NT = (((1,), (1,)), ((), ()))


def mm(a, b, dims=NN, precision=None):
    return lax.dot_general(a, b, dims, precision=precision, preferred_element_type=F32)


def pair(x):
    high = x.astype(BF16).astype(F32)
    return jnp.concatenate([high, x - high], 0).astype(BF16)


def joined(x):
    half = x.shape[0] // 2
    return x[:half] + x[half:]


def kernel(
    grid,
    res_h, old_h, mat_h, fac_h, rig_h, coa_h, onorm,
    p_out, w_out, ab_out,
    resf, oldf, pf, mat, fac, rig, rhalo, nr, coa, table, ubig, m24,
    zb, gat, inner_o, w_o, face_o, face_p, ret_o, ret_p, arc, arz, arp,
    local_sem, halo_send, halo_recv, z_send, z_recv, y_send, y_recv, c_send, c_recv,
    ac_send, ac_recv, az_send, az_recv, ap_send, ap_recv,
):
    nz, ny, nx = grid
    count, cases, half = p_out.shape
    width = 2 * half
    ranks = rig_h.shape[1]
    own_rows = count * ranks
    per_chunk = nz // CHUNKS
    s = lax.axis_index("sub")
    g = lax.axis_index("grp")
    z, y, x, core = s // ny, s % ny, g // 2, g % 2
    groups = 2 * nx
    flat = s * groups + g
    total = nz * ny * groups
    is_first = flat == 0
    is_last = flat == total - 1

    def of_flat(i):
        return (i // groups, i % groups)

    following = of_flat((flat + 1) % total)
    previous = of_flat((flat + total - 1) % total)
    partner = (s, x * 2 + 1 - core)
    line = [(((z + i) % nz) * ny + y, g) for i in range(1, nz)]
    offsets = [(i, j) for i in range(ny) for j in range(nx) if i or j]
    plane = [(z * ny + (y + i) % ny, ((x + j) % nx) * 2 + core) for i, j in offsets]

    def to(src, dst, send, recv, device):
        return pltpu.make_async_remote_copy(
            src_ref=src, dst_ref=dst, send_sem=send, recv_sem=recv,
            device_id=device, device_id_type=pl.DeviceIdType.MESH,
        )

    loads = [
        pltpu.make_async_copy(mat_h, mat, local_sem.at[0]),
        pltpu.make_async_copy(rig_h, rig.at[:, pl.ds(0, ranks), :], local_sem.at[1]),
        pltpu.make_async_copy(res_h, resf.at[pl.ds(1, count)], local_sem.at[2]),
        pltpu.make_async_copy(old_h, oldf.at[pl.ds(1, count)], local_sem.at[3]),
        pltpu.make_async_copy(coa_h, coa.at[pl.ds(8, own_rows)], local_sem.at[4]),
        pltpu.make_async_copy(fac_h, fac, local_sem.at[5]),
    ]
    for load in loads:
        load.start()

    barrier = pltpu.get_barrier_semaphore()
    everyone = [following, previous, partner, *line, *plane]
    for device in everyone:
        pl.semaphore_signal(
            barrier, inc=1, device_id=device, device_id_type=pl.DeviceIdType.MESH
        )

    rig[:, ranks:, :] = jnp.zeros((count, 8 - ranks, width), F32)
    ubig[...] = jnp.zeros_like(ubig)
    pl.semaphore_wait(barrier, len(everyone))

    halo = [
        to(res_h.at[count - 1], resf.at[0], halo_send.at[0], halo_recv.at[0], following),
        to(old_h.at[count - 1], oldf.at[0], halo_send.at[1], halo_recv.at[1], following),
        to(rig_h.at[count - 1, :, pl.ds(half, half)], rhalo, halo_send.at[2], halo_recv.at[2], following),
        to(coa_h.at[pl.ds(own_rows - 8, 8)], coa.at[pl.ds(0, 8)], halo_send.at[3], halo_recv.at[3], following),
        to(coa_h.at[pl.ds(0, 8)], coa.at[pl.ds(8 + own_rows, 8)], halo_send.at[4], halo_recv.at[4], previous),
    ]
    for copy in halo:
        copy.start()

    loads[0].wait()
    unknowns = lax.broadcasted_iota(jnp.int32, (half, half), 0)
    for q in range(count):
        table[q] = jnp.where(unknowns == mat[pl.ds(q, 1), :], -1.0, 0.0).astype(BF16)
    loads[1].wait()
    for q in range(count):
        left = rig[q, :, :half]
        high = left.astype(BF16).astype(F32)
        mid = (left - high).astype(BF16).astype(F32)
        parts = jnp.concatenate([high, mid, left - high - mid], 0).astype(BF16)
        moved = mm(parts, table[q], NT)
        nr[q] = moved[:8] + moved[8:16] + moved[16:]
    to_previous = to(nr.at[0], nr.at[count], halo_send.at[5], halo_recv.at[5], previous)
    to_previous.start()

    loads[2].wait()
    resf[count] = jnp.where(is_last, 0.0, resf[count])
    rights = rig[:, :, half:].reshape(count * 8, half)
    lefts = nr[:count].reshape(count * 8, half)
    own = resf[1:].reshape(count * cases, half)
    sums = mm(rights, own, NT, HIGHEST)
    halo[0].wait_recv()
    resf[0] = jnp.where(is_first, 0.0, resf[0])
    before = resf[:count].reshape(count * cases, half)
    sums = sums + mm(lefts, before, NT, HIGHEST)
    rows = lax.broadcasted_iota(jnp.int32, (count * 8, LANES), 0)
    chunk = lax.broadcasted_iota(jnp.int32, (count * 8, LANES), 1) // cases
    sums = jnp.where(rows // 8 == chunk, sums, 0.0)
    sums = sums + pltpu.roll(sums, LANES // 2, 1)
    sums = sums + pltpu.roll(sums, LANES // 4, 1)
    for q in range(count):
        m24[q * ranks : (q + 1) * ranks, :] = sums[q * 8 : q * 8 + ranks]
    chunk = chunk[:8]
    tile = jnp.zeros((8, LANES), F32)
    for w in range(own_rows // 8):
        tile = jnp.where(chunk == w, m24[w * 8 : (w + 1) * 8, :], tile)
    zb[z] = tile
    z_copies = [to(zb.at[z], zb.at[z], z_send.at[i], z_recv.at[i], d) for i, d in enumerate(line)]
    for copy in z_copies:
        copy.start()

    def interface(field, q):
        left = mm(pair(field[q]), table[q]).astype(BF16)
        return jnp.concatenate([left, pair(field[q + 1])], 1)

    block = width // 4

    def forward(field, q):
        pairs = interface(field, q)
        return jnp.concatenate(
            [
                joined(mm(pairs[:, : (i + 1) * block],
                          fac[q, i * block : (i + 1) * block, : (i + 1) * block], NT))
                for i in range(4)
            ], 1,
        )

    def backward(inner, q):
        pairs = pair(inner)
        solved = jnp.concatenate(
            [
                joined(mm(pairs[:, j * block :], fac[q, j * block :, j * block : (j + 1) * block]))
                for j in range(4)
            ], 1,
        )
        returned = joined(mm(pair(solved[:, :half]), table[q], NT))
        return solved[:, half:], returned

    loads[3].wait()
    halo[1].wait_recv()
    oldf[0] = jnp.where(is_first, 0.0, oldf[0])
    oldf[count] = jnp.where(is_last, 0.0, oldf[count])
    loads[5].wait()
    for q in range(count):
        inner_o[q] = forward(oldf, q)

    for copy in z_copies:
        copy.wait()
    slot = y * nx + x
    for zl in range(per_chunk):
        for w in range(own_rows // 8):
            packed = jnp.zeros((8, LANES), F32)
            for a in range(CHUNKS):
                turned = zb[a * per_chunk + zl]
                if a != w:
                    turned = pltpu.roll(turned, ((a - w) * cases) % LANES, 1)
                packed = jnp.where(chunk == a, turned, packed)
            gat[zl, slot, core, w * 8 : (w + 1) * 8, :] = packed

    def block_of(yx, c):
        return gat.at[:, yx, c]

    y_copies = [
        to(block_of(slot, core), block_of(slot, core), y_send.at[i], y_recv.at[i], d)
        for i, d in enumerate(plane)
    ]
    for copy in y_copies:
        copy.start()
    c_copies = [to(block_of(slot, core), block_of(slot, core), c_send.at[0], c_recv.at[0], partner)]
    c_copies[0].start()

    for q in range(count):
        solved, returned = backward(inner_o[q], q)
        w_o[q] = solved
        if q:
            w_o[q - 1] += returned
        else:
            ret_o[...] = returned
    ret_o_copy = to(ret_o, face_o, halo_send.at[6], halo_recv.at[6], previous)
    ret_o_copy.start()

    halo[2].wait_recv()
    to_previous.wait_recv()
    for f in range(count + 1):
        top = 2 + ranks * f
        columns = pl.ds(f * half, half)
        ubig[top : top + ranks, columns] = rhalo[...] if f == 0 else rig[f - 1, :ranks, half:]
        ubig[top + ranks : top + 2 * ranks, columns] = nr[f, :ranks]
    loads[4].wait()
    halo[3].wait_recv()
    halo[4].wait_recv()

    for i, (copy, (dy, dx)) in enumerate(zip(y_copies, offsets)):
        copy.wait_recv()
        theirs = ((y + ny - dy) % ny) * nx + (x + nx - dx) % nx
        c_copies.append(
            to(block_of(theirs, core), block_of(theirs, core), c_send.at[i + 1], c_recv.at[i + 1], partner)
        )
        c_copies[-1].start()
    for copy in c_copies:
        copy.wait_recv()

    span = coa.shape[1] // CHUNKS
    taken = coa.shape[0]
    stacked = jnp.concatenate([coa[:, a * span : (a + 1) * span] for a in range(CHUNKS)], 0)
    everything = gat[...].reshape(span, LANES)
    products = mm(stacked, everything, NN, HIGHEST)
    chunk_all = lax.broadcasted_iota(jnp.int32, (taken, LANES), 1) // cases
    diagonal = jnp.zeros((taken, LANES), F32)
    for a in range(CHUNKS):
        diagonal = jnp.where(chunk_all == a, products[a * taken : (a + 1) * taken], diagonal)
    diagonal = jnp.concatenate([diagonal, jnp.zeros((LANES - taken, LANES), F32)], 0).T
    coeffs = sum(diagonal[a * cases : (a + 1) * cases] for a in range(CHUNKS))[:, :taken]
    spread = mm(coeffs, ubig[...], NN, HIGHEST)
    norms = jnp.zeros((cases, 1), F32)
    for f in range(count + 1):
        part = resf[f] - spread[:, f * half : (f + 1) * half]
        if f == 0:
            part = jnp.where(is_first, 0.0, part)
        if f == count:
            part = jnp.where(is_last, 0.0, part)
        pf[f] = part
        if f:
            norms = norms + jnp.sum(part * part, 1, keepdims=True)

    inners = [forward(pf, q) for q in range(count)]
    pp, po, oo = (jnp.zeros((cases, 1), F32) for _ in range(3))
    for q in range(count):
        old_inner = inner_o[q]
        pp = pp + jnp.sum(inners[q] * inners[q], 1, keepdims=True)
        po = po + jnp.sum(inners[q] * old_inner, 1, keepdims=True)
        oo = oo + jnp.sum(old_inner * old_inner, 1, keepdims=True)

    lane = lax.broadcasted_iota(jnp.int32, (cases, LANES), 1)
    square = jnp.zeros((cases, LANES), F32)
    for i, column in enumerate((norms, pp, po, oo)):
        square = jnp.where(lane == i, column, square)
    square = jnp.concatenate([square, jnp.zeros((LANES - cases, LANES), F32)], 0).T
    arc[core] = square[:8]
    ac_copy = to(arc.at[core], arc.at[core], ac_send.at[0], ac_recv.at[0], partner)
    ac_copy.start()
    ac_copy.wait()
    arz[z] = arc[0] + arc[1]
    az_copies = [to(arz.at[z], arz.at[z], az_send.at[i], az_recv.at[i], d) for i, d in enumerate(line)]
    for copy in az_copies:
        copy.start()

    for q in range(count):
        solved, returned = backward(inners[q], q)
        w_out[q] = solved
        if q:
            w_out[q - 1] += returned
        else:
            ret_p[...] = returned
            ret_p_copy = to(ret_p, face_p, halo_send.at[7], halo_recv.at[7], previous)
            ret_p_copy.start()
    for copy in az_copies:
        copy.wait()
    arp[slot] = sum(arz[i] for i in range(nz))
    ap_copies = [to(arp.at[slot], arp.at[slot], ap_send.at[i], ap_recv.at[i], d) for i, d in enumerate(plane)]
    for copy in ap_copies:
        copy.start()
    p_out[...] = pf[1:]
    ret_o_copy.wait()
    ret_p_copy.wait()
    w_o[count - 1] = jnp.where(is_last, 0.0, w_o[count - 1] + face_o[...])
    w_out[count - 1] = jnp.where(is_last, 0.0, w_out[count - 1] + face_p[...])
    for copy in ap_copies:
        copy.wait()
    totals = sum(arp[i] for i in range(ny * nx))
    norm = totals[0:1]
    beta = norm / onorm[...]
    curvature = totals[1:2] + 2.0 * beta * totals[2:3] + beta * beta * totals[3:4]
    alpha = norm / curvature
    row = lax.broadcasted_iota(jnp.int32, (LANES, LANES), 0)
    square = jnp.where(row == 0, beta, jnp.where(row == 1, alpha, 0.0)).T
    ab_out[...] = square[:cases]
    column = square[:cases, 0:1]
    for q in range(count):
        w_out[q] += column * w_o[q]

    for copy in halo:
        copy.wait_send()
    to_previous.wait_send()
    for copy in (*y_copies, *c_copies):
        copy.wait_send()


def solution(mesh, ny=4):
    nz, nx = mesh.shape["sub"] // ny, mesh.shape["grp"] // 2
    both = ("sub", "grp")

    def on_device(multipliers, residual, old_direction, old_norms, matching, factor_inverse, rigid_modes, coarse_inverse):
        count, cases, half = multipliers.shape
        ranks = rigid_modes.shape[1]
        own_rows = count * ranks
        width = 2 * half
        coarse = coarse_inverse.shape[1]
        onorm = jnp.concatenate([old_norms, jnp.ones((LANES - cases,), F32)])[None]
        field = jax.ShapeDtypeStruct((count, cases, half), F32)
        dma = pltpu.SemaphoreType.DMA
        scratch = [
            pltpu.VMEM((count + 1, cases, half), F32),
            pltpu.VMEM((count + 1, cases, half), F32),
            pltpu.VMEM((count + 1, cases, half), F32),
            pltpu.VMEM((count, half), jnp.int32),
            pltpu.VMEM((count, width, width), BF16),
            pltpu.VMEM((count, 8, width), F32),
            pltpu.VMEM((ranks, half), F32),
            pltpu.VMEM((count + 1, 8, half), F32),
            pltpu.VMEM((own_rows + 16, coarse), F32),
            pltpu.VMEM((count, half, half), BF16),
            pltpu.VMEM((own_rows + 16, (count + 1) * half), F32),
            pltpu.VMEM((own_rows, LANES), F32),
            pltpu.VMEM((nz, 8, LANES), F32),
            pltpu.VMEM((nz // CHUNKS, ny * nx, 2, own_rows, LANES), F32),
            pltpu.VMEM((count, cases, width), F32),
            pltpu.VMEM((count, cases, half), F32),
            pltpu.VMEM((cases, half), F32),
            pltpu.VMEM((cases, half), F32),
            pltpu.VMEM((cases, half), F32),
            pltpu.VMEM((cases, half), F32),
            pltpu.VMEM((2, 8, LANES), F32),
            pltpu.VMEM((nz, 8, LANES), F32),
            pltpu.VMEM((ny * nx, 8, LANES), F32),
            dma((6,)), dma((8,)), dma((8,)),
            dma((nz - 1,)), dma((nz - 1,)),
            dma((ny * nx - 1,)), dma((ny * nx - 1,)),
            dma((ny * nx,)), dma((ny * nx,)),
            dma((1,)), dma((1,)),
            dma((nz - 1,)), dma((nz - 1,)),
            dma((ny * nx - 1,)), dma((ny * nx - 1,)),
        ]
        projected, image, steps = pl.pallas_call(
            functools.partial(kernel, (nz, ny, nx)),
            out_shape=(field, field, jax.ShapeDtypeStruct((cases, LANES), F32)),
            in_specs=[pl.BlockSpec(memory_space=pl.ANY)] * 6 + [pl.BlockSpec(memory_space=pltpu.VMEM)],
            out_specs=(pl.BlockSpec(memory_space=pltpu.VMEM),) * 3,
            scratch_shapes=scratch,
            compiler_params=pltpu.CompilerParams(
                collective_id=0, has_side_effects=True, vmem_limit_bytes=48 << 20
            ),
        )(residual, old_direction, matching, factor_inverse, rigid_modes, coarse_inverse, onorm)
        flat = lax.axis_index(both) * count + jnp.arange(count, dtype=jnp.int32)
        retain = (flat != count * lax.axis_size(both) - 1).astype(F32)[:, None, None]
        beta, alpha = steps[None, :, 0:1], steps[None, :, 1:2]
        direction = projected + beta * old_direction * retain
        return multipliers + alpha * direction, residual * retain - alpha * image, direction

    fields = P(both, None, None)
    return jax.shard_map(
        on_device,
        mesh=mesh,
        in_specs=(fields, fields, fields, P(), P(both, None), fields, fields, P(both, None)),
        out_specs=(fields, fields, fields),
        check_vma=False,
    )
```

time: 160 us -> 50.6 us (0.32)
  blocking collectives: 90.5 us -> 0 us
  Pallas kernels: 0 us -> 43.2 us
  matrix products: 21.5 us -> 0 us
  starting transfers between devices: 13.8 us -> 0 us
  local copies, waits for them, and re-layouts: 17.8 us -> 5.45 us
  waiting for transfers between devices: 9.25 us -> 0 us
  other arithmetic: 6.11 us -> 0.99 us
    all_to_all x6 -> x0, blocking collectives: 90.5 us -> none  [sent_to_all(): return lax.all_to_all(copies, axis, split_axis=0, concat_axis=0, tiled=True)]
    pallas_call x0 -> x1, Pallas kernels: none -> 43.2 us  [on_device(): pl.pallas_call(functools.partial(kernel, (nz, ny, nx)), out_shape=(field,...]
    dot_general x8 -> x0, matrix products: 21.5 us -> none  [the longest x1 9.82 us: on_device(): jnp.einsum('sci,sij->scj', inner, factor_inverse, preferred_element_type=...]
    ppermute x4 -> x0, starting transfers between devices: 13.8 us -> none  [shifted(): return lax.ppermute(block, axis, route)]
    ppermute x4 -> x0, waiting for transfers between devices: 9.25 us -> none  [shifted(): return lax.ppermute(block, axis, route)]
    transpose x1 -> x0, local copies, waits for them, and re-layouts: 5.2 us -> none  [gathered_by_axis(): blocks = jnp.swapaxes(sent_to_all(leading, near), 0, 1)]
    another operation x1 -> x0, local copies, waits for them, and re-layouts: 4.15 us -> none  [joined_along(): blocks.reshape(*dims[:dim], dims[dim] * dims[dim + 1], *dims[dim + 2:])]
    all_to_all x2 -> x0, other arithmetic: 3.38 us -> none  [sent_to_all(): return lax.all_to_all(copies, axis, split_axis=0, concat_axis=0, tiled=True)]
  transfers between devices with their start and end apart: 4 -> 0, of which waited for: 4 -> 0; matrix products, arithmetic and copies ran while one was open for 0% -> 0% of each run, Pallas kernels for 0% -> 0%
where the time goes in v1:
time: 50.6 us; the launch traced here: 50.4 us
  Pallas kernels  43.2 us (85%)
  local copies, waits for them, and re-layouts  5.45 us (11%)
  other arithmetic  0.99 us (2%)
  between operations  0.68 us (1%)
    pallas_call x1, Pallas kernels, on_device(): pl.pallas_call(functools.partial(kernel, (nz, ny, nx)), out_shape=(field,...  43.2 us
    unnamed x11, local copies, waits for them, and re-layouts  4.61 us

profile of v1, /device:TPU:1, one launch (start us, length us, event | category | flops | bytes accessed | tf_op | source)
XLA Modules:
  0.0 50.4 jit_solution(6556847104192285926)
XLA Ops:
  0.6 0.7 %pad_bitcast_fusion.onorm = f32[1,128]{1,0:T(1,128)S(1)} fusion(f32[32]{0:T(128)} %param.11), kind=kLoop, calls=%fused_computation.6 | loop fusion | bytes 640 | tf_op jit(solution)/shard_map/broadcast_in_dim | solution.py:333
  1.3 1.0 %copy.12.rig_h = f32[4,6,1024]{2,1,0:T(8,128)S(1)} copy(f32[4,6,1024]{2,0,1:T(4,128)} %param.14) | data formatting | bytes 196608 | tf_op args[6]
  2.3 0.0 copy-start
  2.3 0.9 %copy-done = f32[4,32,512]{2,1,0:T(8,128)S(1)} copy-done((f32[4,32,512]{2,1,0:T(8,128)S(1)}, f32[4,32,512]{2,1,0:T(8,128)}, u32[]{:S(2)}) %copy-start) | copy-done | bytes 262168
  3.2 0.0 copy-start.1
  3.2 0.9 %copy-done.1 = f32[4,32,512]{2,1,0:T(8,128)S(1)} copy-done((f32[4,32,512]{2,1,0:T(8,128)S(1)}, f32[4,32,512]{2,1,0:T(8,128)}, u32[]{:S(2)}) %copy-start.1) | copy-done | bytes 262168
  4.2 0.0 copy-start.2
  4.2 1.1 %copy-done.2 = f32[24,6144]{1,0:T(8,128)S(1)} copy-done((f32[24,6144]{1,0:T(8,128)S(1)}, f32[24,6144]{1,0:T(8,128)}, u32[]{:S(2)}) %copy-start.2) | copy-done | bytes 589848
  5.2 0.0 copy-start.3
  5.2 0.7 %copy-done.3 = s32[4,512]{1,0:T(4,128)S(1)} copy-done((s32[4,512]{1,0:T(4,128)S(1)}, s32[4,512]{1,0:T(4,128)}, u32[]{:S(2)}) %copy-start.3) | copy-done | bytes 8216
  5.9 0.0 copy-start.4
  5.9 43.2 %shard_map.103 = (f32[4,32,512]{2,1,0:T(8,128)S(1)}, f32[4,32,512]{2,1,0:T(8,128)S(1)}, f32[32,128]{1,0:T(8,128)S(1)}) custom-call(f32[4,32,512]{2,1,0:T(8,128)S(1)} %copy-done, f32[4,32,512]{2,1,0:T(8,128)S(1)} %copy-done.1, s32[4,512]{1,0:T(4,128)S(1)} %copy-done.3, bf16[4,1024,1024]{2,1,0:T(8,128)(2,1)} %fac_h.1, f32[4,6,1024]{2,1,0:T(8,128)S(1)} %copy.12.rig_h, ...), custom_call_target="tpu_custom_call" | custom-call | tf_op jit(solution)/shard_map/pallas_call | solution.py:368
  49.2 0.2 slice_reduce_fusion.1
  49.4 0.0 copy-done.4
  49.4 1.0 %multiply_add_fusion = (f32[4,32,512]{2,1,0:T(8,128)}, f32[4,32,512]{2,1,0:T(8,128)}, f32[4,32,512]{2,1,0:T(8,128)}) fusion(f32[4,32,512]{2,1,0:T(8,128)S(1)} %copy-done.4, f32[32]{0:T(128)S(1)} %get-tuple-element.9, f32[4,32,512]{2,1,0:T(8,128)S(1)} %get-tuple-element.7, f32[4]{0:T(128)S(1)} %compare_convert_fusion, f32[4,32,512]{2,1,0:T(8,128)S(1)} %copy-done.1, ...), kind=kLoop, calls=%fused_computation.1 | loop fusion | flops 524288 | bytes 2097424 | tf_op jit(solution)/shard_map/add | solution.py:382
  (1 shorter events, 0.0 us)
Async XLA Ops:
  2.3 1.0 %copy-start = (f32[4,32,512]{2,1,0:T(8,128)S(1)}, f32[4,32,512]{2,1,0:T(8,128)}, u32[]{:S(2)}) copy-start(f32[4,32,512]{2,1,0:T(8,128)} %res_h.1) | copy-start | bytes 786436
  3.2 0.9 %copy-start.1 = (f32[4,32,512]{2,1,0:T(8,128)S(1)}, f32[4,32,512]{2,1,0:T(8,128)}, u32[]{:S(2)}) copy-start(f32[4,32,512]{2,1,0:T(8,128)} %old_h.1) | copy-start | bytes 786436
  4.2 1.1 %copy-start.2 = (f32[24,6144]{1,0:T(8,128)S(1)}, f32[24,6144]{1,0:T(8,128)}, u32[]{:S(2)}) copy-start(f32[24,6144]{1,0:T(8,128)} %coa_h.1) | copy-start | bytes 1769476
  5.2 0.7 %copy-start.3 = (s32[4,512]{1,0:T(4,128)S(1)}, s32[4,512]{1,0:T(4,128)}, u32[]{:S(2)}) copy-start(s32[4,512]{1,0:T(4,128)} %mat_h.1) | copy-start | bytes 24580
  5.9 43.4 %copy-start.4 = (f32[4,32,512]{2,1,0:T(8,128)S(1)}, f32[4,32,512]{2,1,0:T(8,128)}, u32[]{:S(2)}) copy-start(f32[4,32,512]{2,1,0:T(8,128)} %param.8) | copy-start | bytes 786436

commit v2 on v1

v2 whole, which is shorter than its diff:
```python
import functools

import jax
import jax.numpy as jnp
from jax import lax
from jax.experimental import pallas as pl
from jax.experimental.pallas import tpu as pltpu
from jax.sharding import PartitionSpec as P

F32 = jnp.float32
BF16 = jnp.bfloat16
HIGHEST = lax.Precision.HIGHEST
CHUNKS = 4
LANES = 128
NN = (((1,), (0,)), ((), ()))
NT = (((1,), (1,)), ((), ()))


def mm(a, b, dims=NN, precision=None):
    return lax.dot_general(a, b, dims, precision=precision, preferred_element_type=F32)


def pair(x):
    high = x.astype(BF16).astype(F32)
    return jnp.concatenate([high, x - high], 0).astype(BF16)


def joined(x):
    half = x.shape[0] // 2
    return x[:half] + x[half:]


def kernel(
    grid,
    res_h, old_h, mat_h, fac_h, rig_h, coa_h, onorm_h,
    p_out, w_out, ab_out,
    resf, oldf, onorm, mat, fac, rigt, rig, rhalo, nr, coa, cpair, table, ubig, lin, m24,
    zb, gat, inner_o, inner_m, w_o, face_o, face_p, ret_o, ret_p, arz, arp,
    local_sem, halo_send, halo_recv, z_send, z_recv, y_send, y_recv, c_send, c_recv,
    az_send, az_recv, ap_send, ap_recv,
):
    nz, ny, nx = grid
    count, cases, half = p_out.shape
    width = 2 * half
    ranks = rig_h.shape[0]
    own_rows = count * ranks
    taken = coa.shape[0]
    span = coa.shape[1] // CHUNKS
    per_chunk = nz // CHUNKS
    s = lax.axis_index("sub")
    g = lax.axis_index("grp")
    z, y, x, core = s // ny, s % ny, g // 2, g % 2
    groups = 2 * nx
    flat = s * groups + g
    total = nz * ny * groups
    is_first = flat == 0
    is_last = flat == total - 1

    def of_flat(i):
        return (i // groups, i % groups)

    following = of_flat((flat + 1) % total)
    previous = of_flat((flat + total - 1) % total)
    partner = (s, x * 2 + 1 - core)
    line = [(((z + i) % nz) * ny + y, g) for i in range(1, nz)]
    across = [(((z + i) % nz) * ny + y, x * 2 + 1 - core) for i in range(1, nz)]
    offsets = [(i, j) for i in range(ny) for j in range(nx) if i or j]
    plane = [(z * ny + (y + i) % ny, ((x + j) % nx) * 2 + core) for i, j in offsets]
    slot = y * nx + x

    def to(src, dst, send, recv, device):
        return pltpu.make_async_remote_copy(
            src_ref=src, dst_ref=dst, send_sem=send, recv_sem=recv,
            device_id=device, device_id_type=pl.DeviceIdType.MESH,
        )

    barrier = pltpu.get_barrier_semaphore()
    everyone = [following, previous, partner, *line, *across, *plane]
    for device in everyone:
        pl.semaphore_signal(
            barrier, inc=1, device_id=device, device_id_type=pl.DeviceIdType.MESH
        )
    loads = [
        pltpu.make_async_copy(mat_h, mat, local_sem.at[0]),
        pltpu.make_async_copy(rig_h, rigt, local_sem.at[1]),
        pltpu.make_async_copy(res_h, resf.at[pl.ds(1, count)], local_sem.at[2]),
        pltpu.make_async_copy(old_h, oldf.at[pl.ds(1, count)], local_sem.at[3]),
        pltpu.make_async_copy(coa_h, coa.at[pl.ds(8, own_rows)], local_sem.at[4]),
        pltpu.make_async_copy(fac_h, fac, local_sem.at[5]),
        pltpu.make_async_copy(onorm_h, onorm, local_sem.at[6]),
    ]
    for load in loads:
        load.start()
    ubig[...] = jnp.zeros_like(ubig)
    lin[...] = jnp.zeros_like(lin)
    rig[:, ranks:, :] = jnp.zeros((count, 8 - ranks, width), F32)

    loads[0].wait()
    unknowns = lax.broadcasted_iota(jnp.int32, (half, half), 0)
    for q in range(count):
        table[q] = jnp.where(unknowns == mat[pl.ds(q, 1), :], -1.0, 0.0).astype(BF16)
    loads[1].wait()
    for q in range(count):
        for m in range(ranks):
            rig[q, m : m + 1, :] = rigt[m, q : q + 1, :]
    for q in range(count):
        left = rig[q, :, :half]
        high = left.astype(BF16).astype(F32)
        mid = (left - high).astype(BF16).astype(F32)
        parts = jnp.concatenate([high, mid, left - high - mid], 0).astype(BF16)
        moved = mm(parts, table[q], NT)
        nr[q] = moved[:8] + moved[8:16] + moved[16:]

    loads[2].wait()
    resf[count] = jnp.where(is_last, 0.0, resf[count])
    rights = rig[:, :, half:].reshape(count * 8, half)
    lefts = nr[:count].reshape(count * 8, half)
    own = resf[1:].reshape(count * cases, half)
    sums = mm(rights, own, NT, HIGHEST)

    pl.semaphore_wait(barrier, len(everyone))
    halo = [
        to(res_h.at[count - 1], resf.at[0], halo_send.at[0], halo_recv.at[0], following),
        to(nr.at[0], nr.at[count], halo_send.at[1], halo_recv.at[1], previous),
        to(rig.at[count - 1, :, pl.ds(half, half)], rhalo, halo_send.at[2], halo_recv.at[2], following),
        to(old_h.at[count - 1], oldf.at[0], halo_send.at[3], halo_recv.at[3], following),
        to(coa_h.at[pl.ds(own_rows - 8, 8)], coa.at[pl.ds(0, 8)], halo_send.at[4], halo_recv.at[4], following),
        to(coa_h.at[pl.ds(0, 8)], coa.at[pl.ds(8 + own_rows, 8)], halo_send.at[5], halo_recv.at[5], previous),
    ]
    for copy in halo:
        copy.start()
    halo[0].wait_recv()
    resf[0] = jnp.where(is_first, 0.0, resf[0])
    before = resf[:count].reshape(count * cases, half)
    sums = sums + mm(lefts, before, NT, HIGHEST)
    rows = lax.broadcasted_iota(jnp.int32, (count * 8, LANES), 0)
    chunk = lax.broadcasted_iota(jnp.int32, (count * 8, LANES), 1) // cases
    sums = jnp.where(rows // 8 == chunk, sums, 0.0)
    sums = sums + pltpu.roll(sums, LANES // 2, 1)
    sums = sums + pltpu.roll(sums, LANES // 4, 1)
    for q in range(count):
        m24[q * ranks : (q + 1) * ranks, :] = sums[q * 8 : q * 8 + ranks]
    chunk = chunk[:8]
    tile = jnp.zeros((8, LANES), F32)
    for w in range(own_rows // 8):
        tile = jnp.where(chunk == w, m24[w * 8 : (w + 1) * 8, :], tile)
    zb[z] = tile
    z_copies = [to(zb.at[z], zb.at[z], z_send.at[i], z_recv.at[i], d) for i, d in enumerate(line)]
    for copy in z_copies:
        copy.start()

    block = width // 4

    def forward(left, right, q):
        pairs = jnp.concatenate([mm(pair(left), table[q]).astype(BF16), pair(right)], 1)
        return jnp.concatenate(
            [
                joined(mm(pairs[:, : (i + 1) * block],
                          fac[q, i * block : (i + 1) * block, : (i + 1) * block], NT))
                for i in range(4)
            ], 1,
        )

    def backward(inner, q):
        pairs = pair(inner)
        solved = jnp.concatenate(
            [
                joined(mm(pairs[:, j * block :], fac[q, j * block :, j * block : (j + 1) * block]))
                for j in range(4)
            ], 1,
        )
        returned = joined(mm(pair(solved[:, :half]), table[q], NT))
        return solved[:, half:], returned

    halo[1].wait_recv()
    halo[2].wait_recv()
    for f in range(count + 1):
        top = 2 + ranks * f
        columns = pl.ds(f * half, half)
        upper = rhalo[:ranks] if f == 0 else rig[f - 1, :ranks, half:]
        lower = nr[f, :ranks]
        if f in (0, count):
            outside = is_last if f else is_first
            upper, lower = jnp.where(outside, 0.0, upper), jnp.where(outside, 0.0, lower)
        ubig[top : top + ranks, columns] = upper
        ubig[top + ranks : top + 2 * ranks, columns] = lower

    def keep(rows_of, values, columns):
        high = values.astype(BF16)
        low = (values - high.astype(F32)).astype(BF16)
        lin[rows_of[0] : rows_of[1], columns] = high
        lin[rows_of[0] + taken : rows_of[1] + taken, columns] = high
        lin[rows_of[0] + 2 * taken : rows_of[1] + 2 * taken, columns] = low

    keep((0, taken), ubig[:, half:], slice(0, count * half))
    loads[3].wait()
    halo[3].wait_recv()
    oldf[0] = jnp.where(is_first, 0.0, oldf[0])
    oldf[count] = jnp.where(is_last, 0.0, oldf[count])
    loads[5].wait()
    for q in range(count):
        low_row = (2 + ranks * q) // 8 * 8
        high_row = -(-(2 + ranks * (q + 3)) // 8) * 8
        sides = [
            jnp.concatenate(
                [oldf[f], resf[f], ubig[low_row:high_row, f * half : (f + 1) * half]], 0
            )
            for f in (q, q + 1)
        ]
        inner = forward(*sides, q)
        inner_o[q] = inner[:cases]
        inner_m[q] = inner[cases : 2 * cases]
        start = count * half + q * width
        keep((low_row, high_row), inner[2 * cases :], slice(start, start + width))

    for copy in z_copies:
        copy.wait()
    for zl in range(per_chunk):
        for w in range(own_rows // 8):
            packed = jnp.zeros((8, LANES), F32)
            for a in range(CHUNKS):
                turned = zb[a * per_chunk + zl]
                if a != w:
                    turned = pltpu.roll(turned, ((a - w) * cases) % LANES, 1)
                packed = jnp.where(chunk == a, turned, packed)
            gat[zl, slot, core, w * 8 : (w + 1) * 8, :] = packed

    def block_of(yx, c):
        return gat.at[:, yx, c]

    y_copies = [
        to(block_of(slot, core), block_of(slot, core), y_send.at[i], y_recv.at[i], d)
        for i, d in enumerate(plane)
    ]
    for copy in y_copies:
        copy.start()
    c_copies = [to(block_of(slot, core), block_of(slot, core), c_send.at[0], c_recv.at[0], partner)]
    c_copies[0].start()

    for q in range(count):
        solved, returned = backward(inner_o[q], q)
        w_o[q] = solved
        if q:
            w_o[q - 1] += returned
        else:
            ret_o[...] = returned
    ret_o_copy = to(ret_o, face_o, halo_send.at[6], halo_recv.at[6], previous)
    ret_o_copy.start()
    loads[4].wait()
    halo[4].wait_recv()
    halo[5].wait_recv()
    for a in range(CHUNKS):
        values = coa[:, a * span : (a + 1) * span]
        high = values.astype(BF16).astype(F32)
        cpair[a * 2 * taken : (a + 1) * 2 * taken] = jnp.concatenate([high, values - high], 0).astype(BF16)

    for i, (copy, (dy, dx)) in enumerate(zip(y_copies, offsets)):
        copy.wait_recv()
        theirs = ((y + ny - dy) % ny) * nx + (x + nx - dx) % nx
        c_copies.append(
            to(block_of(theirs, core), block_of(theirs, core), c_send.at[i + 1], c_recv.at[i + 1], partner)
        )
        c_copies[-1].start()
    for copy in c_copies:
        copy.wait_recv()

    everything = gat[...].reshape(span, LANES)
    high = everything.astype(BF16)
    low = (everything - high.astype(F32)).astype(BF16)
    products = mm(cpair[...], jnp.concatenate([high, low], 1))
    products = products[:, :LANES] + products[:, LANES:]
    chunk_all = lax.broadcasted_iota(jnp.int32, (taken, LANES), 1) // cases
    coeffs = jnp.zeros((taken, LANES), F32)
    for a in range(CHUNKS):
        coeffs = jnp.where(chunk_all == a, joined(products[a * 2 * taken : (a + 1) * 2 * taken]), coeffs)
    coeffs = coeffs + pltpu.roll(coeffs, LANES // 2, 1)
    coeffs = coeffs + pltpu.roll(coeffs, LANES // 4, 1)
    high = coeffs.astype(BF16).astype(F32)
    thrice = jnp.concatenate(
        [high, coeffs - high, high, jnp.zeros((LANES - 3 * taken, LANES), F32)], 0
    ).T[:cases].astype(BF16)
    moved = mm(thrice, lin[...])
    norms, pp, po, oo = (jnp.zeros((cases, 1), F32) for _ in range(4))
    inners = []
    for q in range(count):
        part = resf[q + 1] - moved[:, q * half : (q + 1) * half]
        p_out[q] = part
        start = count * half + q * width
        inner = inner_m[q] - moved[:, start : start + width]
        inners.append(inner)
        old_inner = inner_o[q]
        norms = norms + jnp.sum(part * part, 1, keepdims=True)
        pp = pp + jnp.sum(inner * inner, 1, keepdims=True)
        po = po + jnp.sum(inner * old_inner, 1, keepdims=True)
        oo = oo + jnp.sum(old_inner * old_inner, 1, keepdims=True)

    lane = lax.broadcasted_iota(jnp.int32, (cases, LANES), 1)
    square = jnp.zeros((cases, LANES), F32)
    for i, column in enumerate((norms, pp, po, oo)):
        square = jnp.where(lane == i, column, square)
    square = jnp.concatenate([square, jnp.zeros((LANES - cases, LANES), F32)], 0).T
    here = 2 * z + core
    arz[here] = square[:8]
    az_copies = [
        to(arz.at[here], arz.at[here], az_send.at[i], az_recv.at[i], d)
        for i, d in enumerate([*line, *across, partner])
    ]
    for copy in az_copies:
        copy.start()

    for q in range(count):
        solved, returned = backward(inners[q], q)
        w_out[q] = solved
        if q:
            w_out[q - 1] += returned
        else:
            ret_p[...] = returned
            ret_p_copy = to(ret_p, face_p, halo_send.at[7], halo_recv.at[7], previous)
            ret_p_copy.start()
    for copy in az_copies:
        copy.wait()
    arp[slot] = sum(arz[i] for i in range(2 * nz))
    ap_copies = [to(arp.at[slot], arp.at[slot], ap_send.at[i], ap_recv.at[i], d) for i, d in enumerate(plane)]
    for copy in ap_copies:
        copy.start()
    loads[6].wait()
    ret_o_copy.wait()
    ret_p_copy.wait()
    w_o[count - 1] = jnp.where(is_last, 0.0, w_o[count - 1] + face_o[...])
    w_out[count - 1] = jnp.where(is_last, 0.0, w_out[count - 1] + face_p[...])
    for copy in (*halo, *y_copies, *c_copies):
        copy.wait_send()
    for copy in ap_copies:
        copy.wait()
    totals = sum(arp[i] for i in range(ny * nx))
    norm = totals[0:1]
    beta = norm / jnp.concatenate([onorm[...], jnp.ones((1, LANES - cases), F32)], 1)
    curvature = totals[1:2] + 2.0 * beta * totals[2:3] + beta * beta * totals[3:4]
    alpha = norm / curvature
    row = lax.broadcasted_iota(jnp.int32, (LANES, LANES), 0)
    square = jnp.where(row == 0, beta, jnp.where(row == 1, alpha, 0.0)).T
    ab_out[...] = square[:cases]
    column = square[:cases, 0:1]
    for q in range(count):
        w_out[q] += column * w_o[q]


def solution(mesh, ny=4):
    nz, nx = mesh.shape["sub"] // ny, mesh.shape["grp"] // 2
    both = ("sub", "grp")

    def on_device(multipliers, residual, old_direction, old_norms, matching, factor_inverse, rigid_modes, coarse_inverse):
        count, cases, half = multipliers.shape
        ranks = rigid_modes.shape[1]
        own_rows = count * ranks
        width = 2 * half
        coarse = coarse_inverse.shape[1]
        field = jax.ShapeDtypeStruct((count, cases, half), F32)
        dma = pltpu.SemaphoreType.DMA
        taken = own_rows + 16
        vmem = pltpu.VMEM
        scratch = [
            vmem((count + 1, cases, half), F32),
            vmem((count + 1, cases, half), F32),
            vmem((1, cases), F32),
            vmem((count, half), jnp.int32),
            vmem((count, width, width), BF16),
            vmem((ranks, count, width), F32),
            vmem((count, 8, width), F32),
            vmem((8, half), F32),
            vmem((count + 1, 8, half), F32),
            vmem((taken, coarse), F32),
            vmem((2 * CHUNKS * taken, coarse // CHUNKS), BF16),
            vmem((count, half, half), BF16),
            vmem((taken, (count + 1) * half), F32),
            vmem((LANES, count * (half + width)), BF16),
            vmem((own_rows, LANES), F32),
            vmem((nz, 8, LANES), F32),
            vmem((nz // CHUNKS, ny * nx, 2, own_rows, LANES), F32),
            vmem((count, cases, width), F32),
            vmem((count, cases, width), F32),
            vmem((count, cases, half), F32),
            vmem((cases, half), F32),
            vmem((cases, half), F32),
            vmem((cases, half), F32),
            vmem((cases, half), F32),
            vmem((2 * nz, 8, LANES), F32),
            vmem((ny * nx, 8, LANES), F32),
            dma((7,)), dma((8,)), dma((8,)),
            dma((nz - 1,)), dma((nz - 1,)),
            dma((ny * nx - 1,)), dma((ny * nx - 1,)),
            dma((ny * nx,)), dma((ny * nx,)),
            dma((2 * nz - 1,)), dma((2 * nz - 1,)),
            dma((ny * nx - 1,)), dma((ny * nx - 1,)),
        ]
        projected, image, steps = pl.pallas_call(
            functools.partial(kernel, (nz, ny, nx)),
            out_shape=(field, field, jax.ShapeDtypeStruct((cases, LANES), F32)),
            in_specs=[pl.BlockSpec(memory_space=pltpu.HBM)] * 7,
            out_specs=(pl.BlockSpec(memory_space=pltpu.VMEM),) * 3,
            scratch_shapes=scratch,
            compiler_params=pltpu.CompilerParams(
                collective_id=0, has_side_effects=True, vmem_limit_bytes=48 << 20
            ),
        )(*(pltpu.with_memory_space_constraint(a, pltpu.HBM) for a in (residual, old_direction, matching, factor_inverse, rigid_modes.transpose(1, 0, 2), coarse_inverse, old_norms[None])))
        flat = lax.axis_index(both) * count + jnp.arange(count, dtype=jnp.int32)
        retain = (flat != count * lax.axis_size(both) - 1).astype(F32)[:, None, None]
        beta, alpha = steps[None, :, 0:1], steps[None, :, 1:2]
        direction = projected + beta * old_direction * retain
        return multipliers + alpha * direction, residual * retain - alpha * image, direction

    fields = P(both, None, None)
    return jax.shard_map(
        on_device,
        mesh=mesh,
        in_specs=(fields, fields, fields, P(), P(both, None), fields, fields, P(both, None)),
        out_specs=(fields, fields, fields),
        check_vma=False,
    )
```

time: 50.6 us -> 41.9 us (0.83)
  local copies, waits for them, and re-layouts: 5.45 us -> 0.19 us
  Pallas kernels: 43.2 us -> 39.9 us
    unnamed x11 -> x6, local copies, waits for them, and re-layouts: 4.61 us -> 0.02 us
    pallas_call x1, Pallas kernels: 43.2 us -> 39.9 us  [on_device(): pl.pallas_call(functools.partial(kernel, (nz, ny, nx)), out_shape=(field,...]
    broadcast_in_dim x1 -> x0, local copies, waits for them, and re-layouts: 0.66 us -> none  [on_device(): onorm = jnp.concatenate([old_norms, jnp.ones((LANES - cases,), F32)])[None]]
where the time goes in v2:
time: 41.9 us; the launch traced here: 41.8 us
  Pallas kernels  39.9 us (95%)
  other arithmetic  0.98 us (2%)
  between operations  0.7 us (2%)
    pallas_call x1, Pallas kernels, on_device(): pl.pallas_call(functools.partial(kernel, (nz, ny, nx)), out_shape=(field,...  39.9 us
    add x1, other arithmetic, on_device(): multipliers + alpha * direction  0.98 us

profile of v2, /device:TPU:1, one launch (start us, length us, event | category | flops | bytes accessed | tf_op | source)
XLA Modules:
  0.0 41.8 jit_solution(12998608752298682107)
XLA Ops:
  0.6 0.0 copy-start.1
  0.6 0.0 copy-start
  0.7 0.0 copy-start.2
  0.7 39.9 %shard_map.103 = (f32[4,32,512]{2,1,0:T(8,128)S(1)}, f32[4,32,512]{2,1,0:T(8,128)S(1)}, f32[32,128]{1,0:T(8,128)S(1)}) custom-call(f32[4,32,512]{2,1,0:T(8,128)} %res_h.1, f32[4,32,512]{2,1,0:T(8,128)} %old_h.1, s32[4,512]{1,0:T(4,128)} %mat_h.1, bf16[4,1024,1024]{2,1,0:T(8,128)(2,1)} %fac_h.1, f32[6,4,1024]{2,1,0:T(4,128)} %bitcast.2, f32[24,6144]{1,0:T(8,128)} %coa_h.1, ...), custom_call_target="tpu_custom_call" | custom-call | tf_op jit(solution)/shard_map/pallas_call | solution.py:396
  40.6 0.2 slice_reduce_fusion.1
  40.8 0.0 copy-done.1
  40.8 0.0 copy-done
  40.8 0.0 copy-done.2
  40.8 1.0 %multiply_add_fusion = (f32[4,32,512]{2,1,0:T(8,128)}, f32[4,32,512]{2,1,0:T(8,128)}, f32[4,32,512]{2,1,0:T(8,128)}) fusion(f32[4,32,512]{2,1,0:T(8,128)S(1)} %copy-done.2, f32[32]{0:T(128)S(1)} %get-tuple-element.9, f32[4,32,512]{2,1,0:T(8,128)S(1)} %get-tuple-element.7, f32[4]{0:T(128)S(1)} %compare_convert_fusion, f32[4,32,512]{2,1,0:T(8,128)S(1)} %copy-done.1, ...), kind=kLoop, calls=%fused_computation.1 | loop fusion | flops 524288 | bytes 2097424 | tf_op jit(solution)/shard_map/add | solution.py:410
  (1 shorter events, 0.0 us)
Async XLA Ops:
  0.6 40.1 %copy-start.1 = (f32[4,32,512]{2,1,0:T(8,128)S(1)}, f32[4,32,512]{2,1,0:T(8,128)}, u32[]{:S(2)}) copy-start(f32[4,32,512]{2,1,0:T(8,128)} %old_h.1) | copy-start | bytes 786436
  0.6 40.1 %copy-start = (f32[4,32,512]{2,1,0:T(8,128)S(1)}, f32[4,32,512]{2,1,0:T(8,128)}, u32[]{:S(2)}) copy-start(f32[4,32,512]{2,1,0:T(8,128)} %res_h.1) | copy-start | bytes 786436
  0.7 40.1 %copy-start.2 = (f32[4,32,512]{2,1,0:T(8,128)S(1)}, f32[4,32,512]{2,1,0:T(8,128)}, u32[]{:S(2)}) copy-start(f32[4,32,512]{2,1,0:T(8,128)} %param.8) | copy-start | bytes 786436

commit v3 on v2

--- a/solution.py
+++ b/solution.py
@@ -34,10 +34,10 @@
     grid,
     res_h, old_h, mat_h, fac_h, rig_h, coa_h, onorm_h,
     p_out, w_out, ab_out,
-    resf, oldf, onorm, mat, fac, rigt, rig, rhalo, nr, coa, cpair, table, ubig, lin, m24,
-    zb, gat, inner_o, inner_m, w_o, face_o, face_p, ret_o, ret_p, arz, arp,
+    resf, oldf, onorm, mat, fac, rigt, rig, rhalo, nr, coa, relay, cpair, cpair2, table, ubig, lin, m24,
+    zb, zb2, gat, gat2, inner_o, inner_m, w_o, face_o, face_p, ret_o, ret_p, arz, arp,
     local_sem, halo_send, halo_recv, z_send, z_recv, y_send, y_recv, c_send, c_recv,
-    az_send, az_recv, ap_send, ap_recv,
+    az_send, az_recv, ap_send, ap_recv, z2_send, z2_recv, y2_send, y2_recv, c2_send, c2_recv,
 ):
     nz, ny, nx = grid
     count, cases, half = p_out.shape
@@ -62,9 +62,17 @@
     following = of_flat((flat + 1) % total)
     previous = of_flat((flat + total - 1) % total)
     partner = (s, x * 2 + 1 - core)
-    line = [(((z + i) % nz) * ny + y, g) for i in range(1, nz)]
-    across = [(((z + i) % nz) * ny + y, x * 2 + 1 - core) for i in range(1, nz)]
+    second_next = of_flat((flat + 2) % total)
+    second_previous = of_flat((flat + total - 2) % total)
+    beyond = of_flat((flat + total + 2 - 4 * core) % total)
+    def hops(i, ring):
+        return min(i, ring - i)
+
+    steps = sorted(range(1, nz), key=lambda i: -hops(i, nz))
+    line = [(((z + i) % nz) * ny + y, g) for i in steps]
+    across = [(((z + i) % nz) * ny + y, x * 2 + 1 - core) for i in steps]
     offsets = [(i, j) for i in range(ny) for j in range(nx) if i or j]
+    offsets = sorted(offsets, key=lambda o: -hops(o[0], ny) - hops(o[1], nx))
     plane = [(z * ny + (y + i) % ny, ((x + j) % nx) * 2 + core) for i, j in offsets]
     slot = y * nx + x
 
@@ -74,12 +82,16 @@
             device_id=device, device_id_type=pl.DeviceIdType.MESH,
         )
 
+    def tell(semaphore, device):
+        pl.semaphore_signal(
+            semaphore, inc=1, device_id=device, device_id_type=pl.DeviceIdType.MESH
+        )
+
+    gat2[...] = jnp.zeros_like(gat2)
     barrier = pltpu.get_barrier_semaphore()
-    everyone = [following, previous, partner, *line, *across, *plane]
+    everyone = [*plane, *line, *across, following, previous, partner, second_next, second_previous]
     for device in everyone:
-        pl.semaphore_signal(
-            barrier, inc=1, device_id=device, device_id_type=pl.DeviceIdType.MESH
-        )
+        tell(barrier, device)
     loads = [
         pltpu.make_async_copy(mat_h, mat, local_sem.at[0]),
         pltpu.make_async_copy(rig_h, rigt, local_sem.at[1]),
@@ -111,43 +123,80 @@
         moved = mm(parts, table[q], NT)
         nr[q] = moved[:8] + moved[8:16] + moved[16:]
 
+    rows = lax.broadcasted_iota(jnp.int32, (count * 8, LANES), 0)
+    chunk = lax.broadcasted_iota(jnp.int32, (count * 8, LANES), 1) // cases
     loads[2].wait()
     resf[count] = jnp.where(is_last, 0.0, resf[count])
     rights = rig[:, :, half:].reshape(count * 8, half)
-    lefts = nr[:count].reshape(count * 8, half)
+    lefts = nr[1:count].reshape((count - 1) * 8, half)
     own = resf[1:].reshape(count * cases, half)
     sums = mm(rights, own, NT, HIGHEST)
-
+    before = mm(lefts, own, NT, HIGHEST)
+    before = pltpu.roll(before, cases, 1)
+    before = jnp.concatenate([jnp.zeros((8, LANES), F32), before], 0)
+    sums = jnp.where(rows // 8 == chunk, sums + before, 0.0)
+    sums = sums + pltpu.roll(sums, LANES // 2, 1)
+    sums = sums + pltpu.roll(sums, LANES // 4, 1)
+    for q in range(count):
+        m24[q * ranks : (q + 1) * ranks, :] = sums[q * 8 : q * 8 + ranks]
+    chunk = chunk[:8]
+    tile = jnp.zeros((8, LANES), F32)
+    for w in range(own_rows // 8):
+        tile = jnp.where(chunk == w, m24[w * 8 : (w + 1) * 8, :], tile)
+    faces = jnp.concatenate([pair(resf[count]), jnp.zeros((LANES - 2 * cases, half), BF16)], 0)
+    zb[z] = tile
     pl.semaphore_wait(barrier, len(everyone))
+    inside = pl.multiple_of((1 - core) * (own_rows - 8), 8)
+    edge = pl.multiple_of(core * (own_rows + 8), 8)
     halo = [
         to(res_h.at[count - 1], resf.at[0], halo_send.at[0], halo_recv.at[0], following),
         to(nr.at[0], nr.at[count], halo_send.at[1], halo_recv.at[1], previous),
         to(rig.at[count - 1, :, pl.ds(half, half)], rhalo, halo_send.at[2], halo_recv.at[2], following),
         to(old_h.at[count - 1], oldf.at[0], halo_send.at[3], halo_recv.at[3], following),
-        to(coa_h.at[pl.ds(own_rows - 8, 8)], coa.at[pl.ds(0, 8)], halo_send.at[4], halo_recv.at[4], following),
-        to(coa_h.at[pl.ds(0, 8)], coa.at[pl.ds(8 + own_rows, 8)], halo_send.at[5], halo_recv.at[5], previous),
+        to(coa_h.at[pl.ds(inside, 8)], coa.at[pl.ds(edge, 8)], halo_send.at[4], halo_recv.at[4], partner),
+        to(coa_h.at[pl.ds(own_rows - 8 - inside, 8)], relay, halo_send.at[5], halo_recv.at[5], partner),
     ]
-    for copy in halo:
-        copy.start()
-    halo[0].wait_recv()
-    resf[0] = jnp.where(is_first, 0.0, resf[0])
-    before = resf[:count].reshape(count * cases, half)
-    sums = sums + mm(lefts, before, NT, HIGHEST)
-    rows = lax.broadcasted_iota(jnp.int32, (count * 8, LANES), 0)
-    chunk = lax.broadcasted_iota(jnp.int32, (count * 8, LANES), 1) // cases
-    sums = jnp.where(rows // 8 == chunk, sums, 0.0)
-    sums = sums + pltpu.roll(sums, LANES // 2, 1)
-    sums = sums + pltpu.roll(sums, LANES // 4, 1)
-    for q in range(count):
-        m24[q * ranks : (q + 1) * ranks, :] = sums[q * 8 : q * 8 + ranks]
-    chunk = chunk[:8]
-    tile = jnp.zeros((8, LANES), F32)
-    for w in range(own_rows // 8):
-        tile = jnp.where(chunk == w, m24[w * 8 : (w + 1) * 8, :], tile)
-    zb[z] = tile
-    z_copies = [to(zb.at[z], zb.at[z], z_send.at[i], z_recv.at[i], d) for i, d in enumerate(line)]
-    for copy in z_copies:
-        copy.start()
+    relayed = to(relay, coa.at[pl.ds(edge, 8)], halo_send.at[8], halo_recv.at[8], beyond)
+    halo[1].start()
+
+    def along_line(ref, at, send, recv, devices):
+        copies = [to(ref.at[at], ref.at[at], send.at[i], recv.at[i], d) for i, d in enumerate(devices)]
+        for copy in copies:
+            copy.start()
+        return copies
+
+    def packed(ref, zl, w):
+        block = jnp.zeros((8, LANES), F32)
+        for a in range(CHUNKS):
+            turned = ref[a * per_chunk + zl]
+            if a != w:
+                turned = pltpu.roll(turned, ((a - w) * cases) % LANES, 1)
+            block = jnp.where(chunk == a, turned, block)
+        return block
+
+    def to_plane(ref, depth, send, recv, turn_send, turn_recv):
+        def block(yx):
+            return ref.at[:, yx, core, pl.ds(0, depth)]
+
+        copies = [to(block(slot), block(slot), send.at[i], recv.at[i], d) for i, d in enumerate(plane)]
+        for copy in copies:
+            copy.start()
+        turned = [to(block(slot), block(slot), turn_send.at[0], turn_recv.at[0], partner)]
+        turned[0].start()
+
+        def turn():
+            for i in reversed(range(len(offsets))):
+                dy, dx = offsets[i]
+                copies[i].wait_recv()
+                theirs = block(((y + ny - dy) % ny) * nx + (x + nx - dx) % nx)
+                turned.append(to(theirs, theirs, turn_send.at[i + 1], turn_recv.at[i + 1], partner))
+                turned[-1].start()
+
+        return copies, turned, turn
+
+    z_copies = along_line(zb, z, z_send, z_recv, line)
+    for i in (5, 0, 3, 2, 4):
+        halo[i].start()
 
     block = width // 4
 
@@ -172,18 +221,12 @@
         returned = joined(mm(pair(solved[:, :half]), table[q], NT))
         return solved[:, half:], returned
 
-    halo[1].wait_recv()
-    halo[2].wait_recv()
-    for f in range(count + 1):
-        top = 2 + ranks * f
-        columns = pl.ds(f * half, half)
-        upper = rhalo[:ranks] if f == 0 else rig[f - 1, :ranks, half:]
-        lower = nr[f, :ranks]
+    def place(f, above):
+        top = 2 + ranks * f + (0 if above else ranks)
+        rows_of = (rhalo[:ranks] if f == 0 else rig[f - 1, :ranks, half:]) if above else nr[f, :ranks]
         if f in (0, count):
-            outside = is_last if f else is_first
-            upper, lower = jnp.where(outside, 0.0, upper), jnp.where(outside, 0.0, lower)
-        ubig[top : top + ranks, columns] = upper
-        ubig[top + ranks : top + 2 * ranks, columns] = lower
+            rows_of = jnp.where(is_last if f else is_first, 0.0, rows_of)
+        ubig[top : top + ranks, f * half : (f + 1) * half] = rows_of
 
     def keep(rows_of, values, columns):
         high = values.astype(BF16)
@@ -192,13 +235,7 @@
         lin[rows_of[0] + taken : rows_of[1] + taken, columns] = high
         lin[rows_of[0] + 2 * taken : rows_of[1] + 2 * taken, columns] = low
 
-    keep((0, taken), ubig[:, half:], slice(0, count * half))
-    loads[3].wait()
-    halo[3].wait_recv()
-    oldf[0] = jnp.where(is_first, 0.0, oldf[0])
-    oldf[count] = jnp.where(is_last, 0.0, oldf[count])
-    loads[5].wait()
-    for q in range(count):
+    def apply_all(q):
         low_row = (2 + ranks * q) // 8 * 8
         high_row = -(-(2 + ranks * (q + 3)) // 8) * 8
         sides = [
@@ -213,62 +250,95 @@
         start = count * half + q * width
         keep((low_row, high_row), inner[2 * cases :], slice(start, start + width))
 
-    for copy in z_copies:
+    for f in range(count + 1):
+        if f > 0:
+            place(f, True)
+        if f < count:
+            place(f, False)
+    loads[3].wait()
+    oldf[count] = jnp.where(is_last, 0.0, oldf[count])
+    loads[5].wait()
+    apply_all(1)
+    halo[5].wait_recv()
+    relayed.start()
+    for q in range(2, count - 1):
+        apply_all(q)
+    halo[1].wait_recv()
+    added = mm(pair(nr[count]), faces, NT)
+    added = added[:8] + pltpu.roll(added[:8], LANES - cases, 1) + added[8:]
+    zb2[z] = jnp.where(chunk == 0, added, 0.0)
+    z2_copies = along_line(zb2, z, z2_send, z2_recv, line)
+
+    for copy in reversed(z_copies):
         copy.wait()
     for zl in range(per_chunk):
         for w in range(own_rows // 8):
-            packed = jnp.zeros((8, LANES), F32)
-            for a in range(CHUNKS):
-                turned = zb[a * per_chunk + zl]
-                if a != w:
-                    turned = pltpu.roll(turned, ((a - w) * cases) % LANES, 1)
-                packed = jnp.where(chunk == a, turned, packed)
-            gat[zl, slot, core, w * 8 : (w + 1) * 8, :] = packed
-
-    def block_of(yx, c):
-        return gat.at[:, yx, c]
-
-    y_copies = [
-        to(block_of(slot, core), block_of(slot, core), y_send.at[i], y_recv.at[i], d)
-        for i, d in enumerate(plane)
-    ]
-    for copy in y_copies:
-        copy.start()
-    c_copies = [to(block_of(slot, core), block_of(slot, core), c_send.at[0], c_recv.at[0], partner)]
-    c_copies[0].start()
-
-    for q in range(count):
+            gat[zl, slot, core, w * 8 : (w + 1) * 8, :] = packed(zb, zl, w)
+    y_copies, c_copies, turn = to_plane(gat, own_rows, y_send, y_recv, c_send, c_recv)
+    def take_back(q):
         solved, returned = backward(inner_o[q], q)
-        w_o[q] = solved
-        if q:
+        w_o[q] = solved if q else solved + w_o[0]
+        if q == 1:
+            w_o[0] = returned
+        elif q:
             w_o[q - 1] += returned
         else:
             ret_o[...] = returned
+
+    for q in range(1, count - 1):
+        take_back(q)
+    for copy in reversed(z2_copies):
+        copy.wait()
+    for zl in range(per_chunk):
+        gat2[zl, slot, core, :ranks] = packed(zb2, zl, 0)[:ranks]
+    y2_copies, c2_copies, turn2 = to_plane(gat2, ranks, y2_send, y2_recv, c2_send, c2_recv)
+    halo[0].wait_recv()
+    halo[2].wait_recv()
+    halo[3].wait_recv()
+    resf[0] = jnp.where(is_first, 0.0, resf[0])
+    place(0, True)
+    place(count, False)
+    oldf[0] = jnp.where(is_first, 0.0, oldf[0])
+    for q in (0, count - 1):
+        apply_all(q)
+    keep((0, taken), ubig[:, half:], slice(0, count * half))
+    take_back(0)
     ret_o_copy = to(ret_o, face_o, halo_send.at[6], halo_recv.at[6], previous)
     ret_o_copy.start()
+    take_back(count - 1)
     loads[4].wait()
     halo[4].wait_recv()
-    halo[5].wait_recv()
+    relayed.wait_recv()
+    period = min(LANES // 8 * own_rows, span)
+    kept = period // own_rows * 8
+    source = lax.broadcasted_iota(jnp.int32, (period, kept), 0)
+    target = lax.broadcasted_iota(jnp.int32, (period, kept), 1)
+    chosen = jnp.where(source == target // 8 * own_rows + target % 8, 1.0, 0.0).astype(BF16)
+    following_rows = pltpu.roll(coa[...], coa.shape[1] - own_rows, 1)
     for a in range(CHUNKS):
-        values = coa[:, a * span : (a + 1) * span]
-        high = values.astype(BF16).astype(F32)
-        cpair[a * 2 * taken : (a + 1) * 2 * taken] = jnp.concatenate([high, values - high], 0).astype(BF16)
-
-    for i, (copy, (dy, dx)) in enumerate(zip(y_copies, offsets)):
-        copy.wait_recv()
-        theirs = ((y + ny - dy) % ny) * nx + (x + nx - dx) % nx
-        c_copies.append(
-            to(block_of(theirs, core), block_of(theirs, core), c_send.at[i + 1], c_recv.at[i + 1], partner)
-        )
-        c_copies[-1].start()
+        part = slice(a * span, (a + 1) * span)
+        rows_of = slice(a * 2 * taken, (a + 1) * 2 * taken)
+        cpair[rows_of] = pair(coa[:, part])
+        shifted = pair(following_rows[:, part])
+        cpair2[rows_of] = jnp.concatenate(
+            [mm(shifted[:, k : k + period], chosen) for k in range(0, span, period)], 1
+        ).astype(BF16)
+
+    turn()
+    turn2()
     for copy in c_copies:
         copy.wait_recv()
 
-    everything = gat[...].reshape(span, LANES)
-    high = everything.astype(BF16)
-    low = (everything - high.astype(F32)).astype(BF16)
-    products = mm(cpair[...], jnp.concatenate([high, low], 1))
-    products = products[:, :LANES] + products[:, LANES:]
+    def product(rows_of, gathered):
+        high = gathered.astype(BF16)
+        low = (gathered - high.astype(F32)).astype(BF16)
+        both = mm(rows_of[...], jnp.concatenate([high, low], 1))
+        return both[:, :LANES] + both[:, LANES:]
+
+    products = product(cpair, gat[...].reshape(span, LANES))
+    for copy in c2_copies:
+        copy.wait_recv()
+    products = products + product(cpair2, gat2[...].reshape(span // own_rows * 8, LANES))
     chunk_all = lax.broadcasted_iota(jnp.int32, (taken, LANES), 1) // cases
     coeffs = jnp.zeros((taken, LANES), F32)
     for a in range(CHUNKS):
@@ -300,13 +370,9 @@
         square = jnp.where(lane == i, column, square)
     square = jnp.concatenate([square, jnp.zeros((LANES - cases, LANES), F32)], 0).T
     here = 2 * z + core
-    arz[here] = square[:8]
-    az_copies = [
-        to(arz.at[here], arz.at[here], az_send.at[i], az_recv.at[i], d)
-        for i, d in enumerate([*line, *across, partner])
-    ]
-    for copy in az_copies:
-        copy.start()
+    arz[here] = square[0:1] + sum(pltpu.roll(square[i : i + 1], i * cases, 1) for i in range(1, CHUNKS))
+    pairs_of = [device for both in zip(line, across) for device in both]
+    az_copies = along_line(arz, here, az_send, az_recv, [*pairs_of, partner])
 
     for q in range(count):
         solved, returned = backward(inners[q], q)
@@ -317,29 +383,28 @@
             ret_p[...] = returned
             ret_p_copy = to(ret_p, face_p, halo_send.at[7], halo_recv.at[7], previous)
             ret_p_copy.start()
-    for copy in az_copies:
+    for copy in reversed(az_copies):
         copy.wait()
     arp[slot] = sum(arz[i] for i in range(2 * nz))
-    ap_copies = [to(arp.at[slot], arp.at[slot], ap_send.at[i], ap_recv.at[i], d) for i, d in enumerate(plane)]
-    for copy in ap_copies:
-        copy.start()
+    ap_copies = along_line(arp, slot, ap_send, ap_recv, plane)
     loads[6].wait()
     ret_o_copy.wait()
     ret_p_copy.wait()
     w_o[count - 1] = jnp.where(is_last, 0.0, w_o[count - 1] + face_o[...])
     w_out[count - 1] = jnp.where(is_last, 0.0, w_out[count - 1] + face_p[...])
-    for copy in (*halo, *y_copies, *c_copies):
+    for copy in (*halo, relayed, *y_copies, *c_copies, *y2_copies, *c2_copies):
         copy.wait_send()
-    for copy in ap_copies:
+    for copy in reversed(ap_copies):
         copy.wait()
     totals = sum(arp[i] for i in range(ny * nx))
-    norm = totals[0:1]
+    norm, pure, mixed, old_part = (pltpu.roll(totals, (-i * cases) % LANES, 1) if i else totals for i in range(CHUNKS))
     beta = norm / jnp.concatenate([onorm[...], jnp.ones((1, LANES - cases), F32)], 1)
-    curvature = totals[1:2] + 2.0 * beta * totals[2:3] + beta * beta * totals[3:4]
+    curvature = pure + 2.0 * beta * mixed + beta * beta * old_part
     alpha = norm / curvature
     row = lax.broadcasted_iota(jnp.int32, (LANES, LANES), 0)
     square = jnp.where(row == 0, beta, jnp.where(row == 1, alpha, 0.0)).T
-    ab_out[...] = square[:cases]
+    ab_out[0] = jnp.broadcast_to(square[:cases, 0:1], (cases, half))
+    ab_out[1] = jnp.broadcast_to(square[:cases, 1:2], (cases, half))
     column = square[:cases, 0:1]
     for q in range(count):
         w_out[q] += column * w_o[q]
@@ -370,13 +435,17 @@
             vmem((8, half), F32),
             vmem((count + 1, 8, half), F32),
             vmem((taken, coarse), F32),
+            vmem((8, coarse), F32),
             vmem((2 * CHUNKS * taken, coarse // CHUNKS), BF16),
+            vmem((2 * CHUNKS * taken, coarse // CHUNKS // own_rows * 8), BF16),
             vmem((count, half, half), BF16),
             vmem((taken, (count + 1) * half), F32),
             vmem((LANES, count * (half + width)), BF16),
             vmem((own_rows, LANES), F32),
             vmem((nz, 8, LANES), F32),
+            vmem((nz, 8, LANES), F32),
             vmem((nz // CHUNKS, ny * nx, 2, own_rows, LANES), F32),
+            vmem((nz // CHUNKS, ny * nx, 2, 8, LANES), F32),
             vmem((count, cases, width), F32),
             vmem((count, cases, width), F32),
             vmem((count, cases, half), F32),
@@ -384,18 +453,21 @@
             vmem((cases, half), F32),
             vmem((cases, half), F32),
             vmem((cases, half), F32),
-            vmem((2 * nz, 8, LANES), F32),
-            vmem((ny * nx, 8, LANES), F32),
-            dma((7,)), dma((8,)), dma((8,)),
+            vmem((2 * nz, 1, LANES), F32),
+            vmem((ny * nx, 1, LANES), F32),
+            dma((7,)), dma((9,)), dma((9,)),
             dma((nz - 1,)), dma((nz - 1,)),
             dma((ny * nx - 1,)), dma((ny * nx - 1,)),
             dma((ny * nx,)), dma((ny * nx,)),
             dma((2 * nz - 1,)), dma((2 * nz - 1,)),
             dma((ny * nx - 1,)), dma((ny * nx - 1,)),
+            dma((nz - 1,)), dma((nz - 1,)),
+            dma((ny * nx - 1,)), dma((ny * nx - 1,)),
+            dma((ny * nx,)), dma((ny * nx,)),
         ]
         projected, image, steps = pl.pallas_call(
             functools.partial(kernel, (nz, ny, nx)),
-            out_shape=(field, field, jax.ShapeDtypeStruct((cases, LANES), F32)),
+            out_shape=(field, field, jax.ShapeDtypeStruct((2, cases, half), F32)),
             in_specs=[pl.BlockSpec(memory_space=pltpu.HBM)] * 7,
             out_specs=(pl.BlockSpec(memory_space=pltpu.VMEM),) * 3,
             scratch_shapes=scratch,
@@ -405,7 +477,7 @@
         )(*(pltpu.with_memory_space_constraint(a, pltpu.HBM) for a in (residual, old_direction, matching, factor_inverse, rigid_modes.transpose(1, 0, 2), coarse_inverse, old_norms[None])))
         flat = lax.axis_index(both) * count + jnp.arange(count, dtype=jnp.int32)
         retain = (flat != count * lax.axis_size(both) - 1).astype(F32)[:, None, None]
-        beta, alpha = steps[None, :, 0:1], steps[None, :, 1:2]
+        beta, alpha = steps[0:1], steps[1:2]
         direction = projected + beta * old_direction * retain
         return multipliers + alpha * direction, residual * retain - alpha * image, direction
 

time: 41.9 us -> 39.3 us (0.938)
  Pallas kernels: 39.9 us -> 37.5 us
    pallas_call x1, Pallas kernels: 39.9 us -> 37.5 us  [on_device(): pl.pallas_call(functools.partial(kernel, (nz, ny, nx)), out_shape=(field,...]
where the time goes in v3:
time: 39.3 us
  Pallas kernels  37.5 us (95%)
  other arithmetic  1.02 us (3%)
  between operations  0.71 us (2%)
    pallas_call x1, Pallas kernels, on_device(): pl.pallas_call(functools.partial(kernel, (nz, ny, nx)), out_shape=(field,...  37.5 us
    add x1, other arithmetic, on_device(): multipliers + alpha * direction  1.01 us

profile of v3, /device:TPU:1, one launch (start us, length us, event | category | flops | bytes accessed | tf_op | source)
XLA Modules:
  0.0 39.3 jit_solution(4455862820471725162)
XLA Ops:
  0.6 0.0 copy-start.1
  0.6 0.0 copy-start
  0.7 0.0 copy-start.2
  0.7 37.5 %shard_map.103 = (f32[4,32,512]{2,1,0:T(8,128)S(1)}, f32[4,32,512]{2,1,0:T(8,128)S(1)}, f32[2,32,512]{2,1,0:T(8,128)S(1)}) custom-call(f32[4,32,512]{2,1,0:T(8,128)} %res_h.1, f32[4,32,512]{2,1,0:T(8,128)} %old_h.1, s32[4,512]{1,0:T(4,128)} %mat_h.1, bf16[4,1024,1024]{2,1,0:T(8,128)(2,1)} %fac_h.1, f32[6,4,1024]{2,1,0:T(4,128)} %bitcast.6, ...), custom_call_target="tpu_custom_call" | custom-call | tf_op jit(solution)/shard_map/pallas_call | solution.py:468
  38.2 0.0 copy-done.1
  38.2 0.0 copy-done
  38.2 0.0 copy-done.2
  38.3 1.0 %multiply_add_fusion = (f32[4,32,512]{2,1,0:T(8,128)}, f32[4,32,512]{2,1,0:T(8,128)}, f32[4,32,512]{2,1,0:T(8,128)}) fusion(f32[4,32,512]{2,1,0:T(8,128)S(1)} %copy-done.2, f32[32,512]{1,0:T(8,128)S(1)} %get-tuple-element.12, f32[4,32,512]{2,1,0:T(8,128)S(1)} %get-tuple-element.7, f32[4]{0:T(128)S(1)} %compare_convert_fusion, f32[4,32,512]{2,1,0:T(8,128)S(1)} %copy-done.1, ...), kind=kLoop, calls=%fused_computation.1 | loop fusion | flops 524288 | bytes 2228240 | tf_op jit(solution)/shard_map/add | solution.py:482
  (2 shorter events, 0.0 us)
Async XLA Ops:
  0.6 37.6 %copy-start.1 = (f32[4,32,512]{2,1,0:T(8,128)S(1)}, f32[4,32,512]{2,1,0:T(8,128)}, u32[]{:S(2)}) copy-start(f32[4,32,512]{2,1,0:T(8,128)} %old_h.1) | copy-start | bytes 786436
  0.6 37.6 %copy-start = (f32[4,32,512]{2,1,0:T(8,128)S(1)}, f32[4,32,512]{2,1,0:T(8,128)}, u32[]{:S(2)}) copy-start(f32[4,32,512]{2,1,0:T(8,128)} %res_h.1) | copy-start | bytes 786436
  0.7 37.6 %copy-start.2 = (f32[4,32,512]{2,1,0:T(8,128)S(1)}, f32[4,32,512]{2,1,0:T(8,128)}, u32[]{:S(2)}) copy-start(f32[4,32,512]{2,1,0:T(8,128)} %param.8) | copy-start | bytes 786436

commit v4 on v3

--- a/solution.py
+++ b/solution.py
@@ -157,7 +157,11 @@
         to(coa_h.at[pl.ds(own_rows - 8 - inside, 8)], relay, halo_send.at[5], halo_recv.at[5], partner),
     ]
     relayed = to(relay, coa.at[pl.ds(edge, 8)], halo_send.at[8], halo_recv.at[8], beyond)
-    halo[1].start()
+
+    @pl.when(jnp.logical_not(is_first))
+    def _():
+        halo[1].start()
+
 
     def along_line(ref, at, send, recv, devices):
         copies = [to(ref.at[at], ref.at[at], send.at[i], recv.at[i], d) for i, d in enumerate(devices)]
@@ -263,18 +267,28 @@
     relayed.start()
     for q in range(2, count - 1):
         apply_all(q)
-    halo[1].wait_recv()
-    added = mm(pair(nr[count]), faces, NT)
-    added = added[:8] + pltpu.roll(added[:8], LANES - cases, 1) + added[8:]
-    zb2[z] = jnp.where(chunk == 0, added, 0.0)
-    z2_copies = along_line(zb2, z, z2_send, z2_recv, line)
-
+    z2_copies = [to(zb2.at[z], zb2.at[z], z2_send.at[i], z2_recv.at[i], d) for i, d in enumerate(line)]
+
+    def send_corrections():
+        @pl.when(jnp.logical_not(is_last))
+        def _():
+            halo[1].wait_recv()
+
+        added = mm(pair(jnp.where(is_last, 0.0, nr[count])), faces, NT)
+        added = added[:8] + pltpu.roll(added[:8], LANES - cases, 1) + added[8:]
+        zb2[z] = jnp.where(chunk == 0, added, 0.0)
+        for copy in z2_copies:
+            copy.start()
+
+    far_next = jnp.logical_and(jnp.logical_and(x == nx - 1, y == ny - 1), core == 1)
+    pl.when(jnp.logical_not(far_next))(send_corrections)
     for copy in reversed(z_copies):
         copy.wait()
     for zl in range(per_chunk):
         for w in range(own_rows // 8):
             gat[zl, slot, core, w * 8 : (w + 1) * 8, :] = packed(zb, zl, w)
     y_copies, c_copies, turn = to_plane(gat, own_rows, y_send, y_recv, c_send, c_recv)
+    pl.when(far_next)(send_corrections)
     def take_back(q):
         solved, returned = backward(inner_o[q], q)
         w_o[q] = solved if q else solved + w_o[0]
@@ -392,7 +406,11 @@
     ret_p_copy.wait()
     w_o[count - 1] = jnp.where(is_last, 0.0, w_o[count - 1] + face_o[...])
     w_out[count - 1] = jnp.where(is_last, 0.0, w_out[count - 1] + face_p[...])
-    for copy in (*halo, relayed, *y_copies, *c_copies, *y2_copies, *c2_copies):
+    @pl.when(jnp.logical_not(is_first))
+    def _():
+        halo[1].wait_send()
+
+    for copy in (halo[0], *halo[2:], relayed, *y_copies, *c_copies, *y2_copies, *c2_copies):
         copy.wait_send()
     for copy in reversed(ap_copies):
         copy.wait()

time: 39.3 us -> 39.3 us (level)
  no operation moved by 1% of the time
where the time goes in v4:
time: 39.3 us; the launch traced here: 39.2 us
  Pallas kernels  37.5 us (95%)
  other arithmetic  1.02 us (3%)
  between operations  0.71 us (2%)
    pallas_call x1, Pallas kernels, on_device(): pl.pallas_call(functools.partial(kernel, (nz, ny, nx)), out_shape=(field,...  37.5 us
    add x1, other arithmetic, on_device(): multipliers + alpha * direction  1.01 us

profile of v4, /device:TPU:1, one launch (start us, length us, event | category | flops | bytes accessed | tf_op | source)
XLA Modules:
  0.0 39.2 jit_solution(9610509609800622944)
XLA Ops:
  0.6 0.0 copy-start.1
  0.6 0.0 copy-start
  0.7 0.0 copy-start.2
  0.7 37.5 %shard_map.103 = (f32[4,32,512]{2,1,0:T(8,128)S(1)}, f32[4,32,512]{2,1,0:T(8,128)S(1)}, f32[2,32,512]{2,1,0:T(8,128)S(1)}) custom-call(f32[4,32,512]{2,1,0:T(8,128)} %res_h.1, f32[4,32,512]{2,1,0:T(8,128)} %old_h.1, s32[4,512]{1,0:T(4,128)} %mat_h.1, bf16[4,1024,1024]{2,1,0:T(8,128)(2,1)} %fac_h.1, f32[6,4,1024]{2,1,0:T(4,128)} %bitcast.6, ...), custom_call_target="tpu_custom_call" | custom-call | tf_op jit(solution)/shard_map/pallas_call | solution.py:486
  38.2 0.0 copy-done.1
  38.2 0.0 copy-done
  38.2 0.0 copy-done.2
  38.2 1.0 %multiply_add_fusion = (f32[4,32,512]{2,1,0:T(8,128)}, f32[4,32,512]{2,1,0:T(8,128)}, f32[4,32,512]{2,1,0:T(8,128)}) fusion(f32[4,32,512]{2,1,0:T(8,128)S(1)} %copy-done.2, f32[32,512]{1,0:T(8,128)S(1)} %get-tuple-element.12, f32[4,32,512]{2,1,0:T(8,128)S(1)} %get-tuple-element.7, f32[4]{0:T(128)S(1)} %compare_convert_fusion, f32[4,32,512]{2,1,0:T(8,128)S(1)} %copy-done.1, ...), kind=kLoop, calls=%fused_computation.1 | loop fusion | flops 524288 | bytes 2228240 | tf_op jit(solution)/shard_map/add | solution.py:500
  (2 shorter events, 0.0 us)
Async XLA Ops:
  0.6 37.6 %copy-start.1 = (f32[4,32,512]{2,1,0:T(8,128)S(1)}, f32[4,32,512]{2,1,0:T(8,128)}, u32[]{:S(2)}) copy-start(f32[4,32,512]{2,1,0:T(8,128)} %old_h.1) | copy-start | bytes 786436
  0.6 37.6 %copy-start = (f32[4,32,512]{2,1,0:T(8,128)S(1)}, f32[4,32,512]{2,1,0:T(8,128)}, u32[]{:S(2)}) copy-start(f32[4,32,512]{2,1,0:T(8,128)} %res_h.1) | copy-start | bytes 786436
  0.7 37.6 %copy-start.2 = (f32[4,32,512]{2,1,0:T(8,128)S(1)}, f32[4,32,512]{2,1,0:T(8,128)}, u32[]{:S(2)}) copy-start(f32[4,32,512]{2,1,0:T(8,128)} %param.8) | copy-start | bytes 786436

commit v5 on v4

--- a/solution.py
+++ b/solution.py
@@ -34,7 +34,7 @@
     grid,
     res_h, old_h, mat_h, fac_h, rig_h, coa_h, onorm_h,
     p_out, w_out, ab_out,
-    resf, oldf, onorm, mat, fac, rigt, rig, rhalo, nr, coa, relay, cpair, cpair2, table, ubig, lin, m24,
+    resf, oldf, onorm, mat, fac, rigt, rig, rhalo, nr, coa, rows_in, rows_out, relay, cpair, cpair2, table, ubig, lin, m24,
     zb, zb2, gat, gat2, inner_o, inner_m, w_o, face_o, face_p, ret_o, ret_p, arz, arp,
     local_sem, halo_send, halo_recv, z_send, z_recv, y_send, y_recv, c_send, c_recv,
     az_send, az_recv, ap_send, ap_recv, z2_send, z2_recv, y2_send, y2_recv, c2_send, c2_recv,
@@ -44,8 +44,8 @@
     width = 2 * half
     ranks = rig_h.shape[0]
     own_rows = count * ranks
-    taken = coa.shape[0]
-    span = coa.shape[1] // CHUNKS
+    taken = 8 * coa.shape[0]
+    span = coa.shape[2] // CHUNKS
     per_chunk = nz // CHUNKS
     s = lax.axis_index("sub")
     g = lax.axis_index("grp")
@@ -88,6 +88,8 @@
         )
 
     gat2[...] = jnp.zeros_like(gat2)
+    for end in (0, coa.shape[0] - 1):
+        coa[end] = jnp.zeros(coa.shape[1:], F32)
     barrier = pltpu.get_barrier_semaphore()
     everyone = [*plane, *line, *across, following, previous, partner, second_next, second_previous]
     for device in everyone:
@@ -97,7 +99,7 @@
         pltpu.make_async_copy(rig_h, rigt, local_sem.at[1]),
         pltpu.make_async_copy(res_h, resf.at[pl.ds(1, count)], local_sem.at[2]),
         pltpu.make_async_copy(old_h, oldf.at[pl.ds(1, count)], local_sem.at[3]),
-        pltpu.make_async_copy(coa_h, coa.at[pl.ds(8, own_rows)], local_sem.at[4]),
+        pltpu.make_async_copy(coa_h, coa.at[pl.ds(1, own_rows // 8)], local_sem.at[4]),
         pltpu.make_async_copy(fac_h, fac, local_sem.at[5]),
         pltpu.make_async_copy(onorm_h, onorm, local_sem.at[6]),
     ]
@@ -145,29 +147,36 @@
         tile = jnp.where(chunk == w, m24[w * 8 : (w + 1) * 8, :], tile)
     faces = jnp.concatenate([pair(resf[count]), jnp.zeros((LANES - 2 * cases, half), BF16)], 0)
     zb[z] = tile
+    loads[4].wait()
+    firsts, lasts = coa[1], pltpu.roll(coa[coa.shape[0] - 2], ranks, 0)
+    rows_in[...] = jnp.where(core == 1, firsts, lasts)
+    rows_out[...] = jnp.where(core == 1, lasts, firsts)
     pl.semaphore_wait(barrier, len(everyone))
-    inside = pl.multiple_of((1 - core) * (own_rows - 8), 8)
-    edge = pl.multiple_of(core * (own_rows + 8), 8)
+    edge = core * (coa.shape[0] - 1)
+    some = pl.ds(0, ranks)
     halo = [
         to(res_h.at[count - 1], resf.at[0], halo_send.at[0], halo_recv.at[0], following),
         to(nr.at[0], nr.at[count], halo_send.at[1], halo_recv.at[1], previous),
         to(rig.at[count - 1, :, pl.ds(half, half)], rhalo, halo_send.at[2], halo_recv.at[2], following),
         to(old_h.at[count - 1], oldf.at[0], halo_send.at[3], halo_recv.at[3], following),
-        to(coa_h.at[pl.ds(inside, 8)], coa.at[pl.ds(edge, 8)], halo_send.at[4], halo_recv.at[4], partner),
-        to(coa_h.at[pl.ds(own_rows - 8 - inside, 8)], relay, halo_send.at[5], halo_recv.at[5], partner),
+        to(rows_in.at[some], coa.at[edge, some], halo_send.at[4], halo_recv.at[4], partner),
+        to(rows_out.at[some], relay.at[some], halo_send.at[5], halo_recv.at[5], partner),
     ]
-    relayed = to(relay, coa.at[pl.ds(edge, 8)], halo_send.at[8], halo_recv.at[8], beyond)
+    relayed = to(relay.at[some], coa.at[edge, some], halo_send.at[8], halo_recv.at[8], beyond)
 
     @pl.when(jnp.logical_not(is_first))
     def _():
         halo[1].start()
 
 
+    def all_of(ref, number, send, recv):
+        whole = ref.at[pl.ds(0, number)]
+        return to(whole, whole, send, recv, partner)
+
     def along_line(ref, at, send, recv, devices):
-        copies = [to(ref.at[at], ref.at[at], send.at[i], recv.at[i], d) for i, d in enumerate(devices)]
-        for copy in copies:
-            copy.start()
-        return copies
+        for device in devices:
+            to(ref.at[at], ref.at[at], send, recv, device).start()
+        return all_of(ref, len(devices), send, recv)
 
     def packed(ref, zl, w):
         block = jnp.zeros((8, LANES), F32)
@@ -182,21 +191,21 @@
         def block(yx):
             return ref.at[:, yx, core, pl.ds(0, depth)]
 
-        copies = [to(block(slot), block(slot), send.at[i], recv.at[i], d) for i, d in enumerate(plane)]
+        copies = [to(block(slot), block(slot), send, recv.at[i], d) for i, d in enumerate(plane)]
         for copy in copies:
             copy.start()
-        turned = [to(block(slot), block(slot), turn_send.at[0], turn_recv.at[0], partner)]
-        turned[0].start()
+        to(block(slot), block(slot), turn_send, turn_recv, partner).start()
 
         def turn():
             for i in reversed(range(len(offsets))):
                 dy, dx = offsets[i]
                 copies[i].wait_recv()
                 theirs = block(((y + ny - dy) % ny) * nx + (x + nx - dx) % nx)
-                turned.append(to(theirs, theirs, turn_send.at[i + 1], turn_recv.at[i + 1], partner))
-                turned[-1].start()
-
-        return copies, turned, turn
+                to(theirs, theirs, turn_send, turn_recv, partner).start()
+
+        sent = ref.at[:, pl.ds(0, len(plane)), 0, pl.ds(0, depth)]
+        both = ref.at[:, :, 0, pl.ds(0, depth)]
+        return to(sent, sent, send, recv.at[0], partner), to(both, both, turn_send, turn_recv, partner), turn
 
     z_copies = along_line(zb, z, z_send, z_recv, line)
     for i in (5, 0, 3, 2, 4):
@@ -226,7 +235,7 @@
         return solved[:, half:], returned
 
     def place(f, above):
-        top = 2 + ranks * f + (0 if above else ranks)
+        top = (2 + ranks * f if f else 0) if above else 2 + ranks * (f + 1)
         rows_of = (rhalo[:ranks] if f == 0 else rig[f - 1, :ranks, half:]) if above else nr[f, :ranks]
         if f in (0, count):
             rows_of = jnp.where(is_last if f else is_first, 0.0, rows_of)
@@ -267,7 +276,6 @@
     relayed.start()
     for q in range(2, count - 1):
         apply_all(q)
-    z2_copies = [to(zb2.at[z], zb2.at[z], z2_send.at[i], z2_recv.at[i], d) for i, d in enumerate(line)]
 
     def send_corrections():
         @pl.when(jnp.logical_not(is_last))
@@ -277,13 +285,12 @@
         added = mm(pair(jnp.where(is_last, 0.0, nr[count])), faces, NT)
         added = added[:8] + pltpu.roll(added[:8], LANES - cases, 1) + added[8:]
         zb2[z] = jnp.where(chunk == 0, added, 0.0)
-        for copy in z2_copies:
-            copy.start()
+        for device in line:
+            to(zb2.at[z], zb2.at[z], z2_send, z2_recv, device).start()
 
     far_next = jnp.logical_and(jnp.logical_and(x == nx - 1, y == ny - 1), core == 1)
     pl.when(jnp.logical_not(far_next))(send_corrections)
-    for copy in reversed(z_copies):
-        copy.wait()
+    z_copies.wait()
     for zl in range(per_chunk):
         for w in range(own_rows // 8):
             gat[zl, slot, core, w * 8 : (w + 1) * 8, :] = packed(zb, zl, w)
@@ -301,8 +308,7 @@
 
     for q in range(1, count - 1):
         take_back(q)
-    for copy in reversed(z2_copies):
-        copy.wait()
+    all_of(zb2, len(line), z2_send, z2_recv).wait()
     for zl in range(per_chunk):
         gat2[zl, slot, core, :ranks] = packed(zb2, zl, 0)[:ranks]
     y2_copies, c2_copies, turn2 = to_plane(gat2, ranks, y2_send, y2_recv, c2_send, c2_recv)
@@ -320,7 +326,6 @@
     ret_o_copy = to(ret_o, face_o, halo_send.at[6], halo_recv.at[6], previous)
     ret_o_copy.start()
     take_back(count - 1)
-    loads[4].wait()
     halo[4].wait_recv()
     relayed.wait_recv()
     period = min(LANES // 8 * own_rows, span)
@@ -328,11 +333,12 @@
     source = lax.broadcasted_iota(jnp.int32, (period, kept), 0)
     target = lax.broadcasted_iota(jnp.int32, (period, kept), 1)
     chosen = jnp.where(source == target // 8 * own_rows + target % 8, 1.0, 0.0).astype(BF16)
-    following_rows = pltpu.roll(coa[...], coa.shape[1] - own_rows, 1)
+    coarse_rows = coa[...].reshape(taken, CHUNKS * span)
+    following_rows = pltpu.roll(coarse_rows, CHUNKS * span - own_rows, 1)
     for a in range(CHUNKS):
         part = slice(a * span, (a + 1) * span)
         rows_of = slice(a * 2 * taken, (a + 1) * 2 * taken)
-        cpair[rows_of] = pair(coa[:, part])
+        cpair[rows_of] = pair(coarse_rows[:, part])
         shifted = pair(following_rows[:, part])
         cpair2[rows_of] = jnp.concatenate(
             [mm(shifted[:, k : k + period], chosen) for k in range(0, span, period)], 1
@@ -340,8 +346,7 @@
 
     turn()
     turn2()
-    for copy in c_copies:
-        copy.wait_recv()
+    c_copies.wait_recv()
 
     def product(rows_of, gathered):
         high = gathered.astype(BF16)
@@ -350,8 +355,7 @@
         return both[:, :LANES] + both[:, LANES:]
 
     products = product(cpair, gat[...].reshape(span, LANES))
-    for copy in c2_copies:
-        copy.wait_recv()
+    c2_copies.wait_recv()
     products = products + product(cpair2, gat2[...].reshape(span // own_rows * 8, LANES))
     chunk_all = lax.broadcasted_iota(jnp.int32, (taken, LANES), 1) // cases
     coeffs = jnp.zeros((taken, LANES), F32)
@@ -397,8 +401,7 @@
             ret_p[...] = returned
             ret_p_copy = to(ret_p, face_p, halo_send.at[7], halo_recv.at[7], previous)
             ret_p_copy.start()
-    for copy in reversed(az_copies):
-        copy.wait()
+    az_copies.wait()
     arp[slot] = sum(arz[i] for i in range(2 * nz))
     ap_copies = along_line(arp, slot, ap_send, ap_recv, plane)
     loads[6].wait()
@@ -410,10 +413,9 @@
     def _():
         halo[1].wait_send()
 
-    for copy in (halo[0], *halo[2:], relayed, *y_copies, *c_copies, *y2_copies, *c2_copies):
+    for copy in (halo[0], *halo[2:], relayed, y_copies, c_copies, y2_copies, c2_copies):
         copy.wait_send()
-    for copy in reversed(ap_copies):
-        copy.wait()
+    ap_copies.wait()
     totals = sum(arp[i] for i in range(ny * nx))
     norm, pure, mixed, old_part = (pltpu.roll(totals, (-i * cases) % LANES, 1) if i else totals for i in range(CHUNKS))
     beta = norm / jnp.concatenate([onorm[...], jnp.ones((1, LANES - cases), F32)], 1)
@@ -452,7 +454,9 @@
             vmem((count, 8, width), F32),
             vmem((8, half), F32),
             vmem((count + 1, 8, half), F32),
-            vmem((taken, coarse), F32),
+            vmem((taken // 8, 8, coarse), F32),
+            vmem((8, coarse), F32),
+            vmem((8, coarse), F32),
             vmem((8, coarse), F32),
             vmem((2 * CHUNKS * taken, coarse // CHUNKS), BF16),
             vmem((2 * CHUNKS * taken, coarse // CHUNKS // own_rows * 8), BF16),
@@ -474,14 +478,9 @@
             vmem((2 * nz, 1, LANES), F32),
             vmem((ny * nx, 1, LANES), F32),
             dma((7,)), dma((9,)), dma((9,)),
-            dma((nz - 1,)), dma((nz - 1,)),
-            dma((ny * nx - 1,)), dma((ny * nx - 1,)),
-            dma((ny * nx,)), dma((ny * nx,)),
-            dma((2 * nz - 1,)), dma((2 * nz - 1,)),
-            dma((ny * nx - 1,)), dma((ny * nx - 1,)),
-            dma((nz - 1,)), dma((nz - 1,)),
-            dma((ny * nx - 1,)), dma((ny * nx - 1,)),
-            dma((ny * nx,)), dma((ny * nx,)),
+            dma, dma, dma, dma((ny * nx - 1,)), dma, dma,
+            dma, dma, dma, dma,
+            dma, dma, dma, dma((ny * nx - 1,)), dma, dma,
         ]
         projected, image, steps = pl.pallas_call(
             functools.partial(kernel, (nz, ny, nx)),
@@ -492,7 +491,7 @@
             compiler_params=pltpu.CompilerParams(
                 collective_id=0, has_side_effects=True, vmem_limit_bytes=48 << 20
             ),
-        )(*(pltpu.with_memory_space_constraint(a, pltpu.HBM) for a in (residual, old_direction, matching, factor_inverse, rigid_modes.transpose(1, 0, 2), coarse_inverse, old_norms[None])))
+        )(*(pltpu.with_memory_space_constraint(a, pltpu.HBM) for a in (residual, old_direction, matching, factor_inverse, rigid_modes.transpose(1, 0, 2), coarse_inverse.reshape(own_rows // 8, 8, coarse), old_norms[None])))
         flat = lax.axis_index(both) * count + jnp.arange(count, dtype=jnp.int32)
         retain = (flat != count * lax.axis_size(both) - 1).astype(F32)[:, None, None]
         beta, alpha = steps[0:1], steps[1:2]

time: 39.3 us -> 36.7 us (0.934)
  Pallas kernels: 37.5 us -> 34.9 us
    pallas_call x1, Pallas kernels: 37.5 us -> 34.9 us  [on_device(): pl.pallas_call(functools.partial(kernel, (nz, ny, nx)), out_shape=(field,...]
where the time goes in v5:
time: 36.7 us
  Pallas kernels  34.9 us (95%)
  other arithmetic  1.02 us (3%)
  between operations  0.71 us (2%)
    pallas_call x1, Pallas kernels, on_device(): pl.pallas_call(functools.partial(kernel, (nz, ny, nx)), out_shape=(field,...  34.9 us
    add x1, other arithmetic, on_device(): multipliers + alpha * direction  1.01 us

profile of v5, /device:TPU:1, one launch (start us, length us, event | category | flops | bytes accessed | tf_op | source)
XLA Modules:
  0.0 36.7 jit_solution(4954478043296474649)
XLA Ops:
  0.6 0.0 copy-start.1
  0.6 0.0 copy-start
  0.7 0.0 copy-start.2
  0.7 34.9 %shard_map.103 = (f32[4,32,512]{2,1,0:T(8,128)S(1)}, f32[4,32,512]{2,1,0:T(8,128)S(1)}, f32[2,32,512]{2,1,0:T(8,128)S(1)}) custom-call(f32[4,32,512]{2,1,0:T(8,128)} %res_h.1, f32[4,32,512]{2,1,0:T(8,128)} %old_h.1, s32[4,512]{1,0:T(4,128)} %mat_h.1, bf16[4,1024,1024]{2,1,0:T(8,128)(2,1)} %fac_h.1, f32[6,4,1024]{2,1,0:T(4,128)} %bitcast.8, ...), custom_call_target="tpu_custom_call" | custom-call | tf_op jit(solution)/shard_map/pallas_call | solution.py:485
  35.6 0.0 copy-done.1
  35.6 0.0 copy-done
  35.6 0.0 copy-done.2
  35.7 1.0 %multiply_add_fusion = (f32[4,32,512]{2,1,0:T(8,128)}, f32[4,32,512]{2,1,0:T(8,128)}, f32[4,32,512]{2,1,0:T(8,128)}) fusion(f32[4,32,512]{2,1,0:T(8,128)S(1)} %copy-done.2, f32[32,512]{1,0:T(8,128)S(1)} %get-tuple-element.12, f32[4,32,512]{2,1,0:T(8,128)S(1)} %get-tuple-element.7, f32[4]{0:T(128)S(1)} %compare_convert_fusion, f32[4,32,512]{2,1,0:T(8,128)S(1)} %copy-done.1, ...), kind=kLoop, calls=%fused_computation.1 | loop fusion | flops 524288 | bytes 2228240 | tf_op jit(solution)/shard_map/add | solution.py:499
  (2 shorter events, 0.0 us)
Async XLA Ops:
  0.6 35.0 %copy-start.1 = (f32[4,32,512]{2,1,0:T(8,128)S(1)}, f32[4,32,512]{2,1,0:T(8,128)}, u32[]{:S(2)}) copy-start(f32[4,32,512]{2,1,0:T(8,128)} %old_h.1) | copy-start | bytes 786436
  0.6 35.0 %copy-start = (f32[4,32,512]{2,1,0:T(8,128)S(1)}, f32[4,32,512]{2,1,0:T(8,128)}, u32[]{:S(2)}) copy-start(f32[4,32,512]{2,1,0:T(8,128)} %res_h.1) | copy-start | bytes 786436
  0.7 35.0 %copy-start.2 = (f32[4,32,512]{2,1,0:T(8,128)S(1)}, f32[4,32,512]{2,1,0:T(8,128)}, u32[]{:S(2)}) copy-start(f32[4,32,512]{2,1,0:T(8,128)} %param.8) | copy-start | bytes 786436

commit v6 on v5

--- a/solution.py
+++ b/solution.py
@@ -73,6 +73,7 @@
     across = [(((z + i) % nz) * ny + y, x * 2 + 1 - core) for i in steps]
     offsets = [(i, j) for i in range(ny) for j in range(nx) if i or j]
     offsets = sorted(offsets, key=lambda o: -hops(o[0], ny) - hops(o[1], nx))
+    rings = [hops(i, ny) + hops(j, nx) for i, j in offsets]
     plane = [(z * ny + (y + i) % ny, ((x + j) % nx) * 2 + core) for i, j in offsets]
     slot = y * nx + x
 
@@ -191,17 +192,18 @@
         def block(yx):
             return ref.at[:, yx, core, pl.ds(0, depth)]
 
-        copies = [to(block(slot), block(slot), send, recv.at[i], d) for i, d in enumerate(plane)]
-        for copy in copies:
-            copy.start()
+        for device, ring in zip(plane, rings):
+            to(block(slot), block(slot), send, recv.at[ring - 1], device).start()
         to(block(slot), block(slot), turn_send, turn_recv, partner).start()
 
         def turn():
-            for i in reversed(range(len(offsets))):
-                dy, dx = offsets[i]
-                copies[i].wait_recv()
-                theirs = block(((y + ny - dy) % ny) * nx + (x + nx - dx) % nx)
-                to(theirs, theirs, turn_send, turn_recv, partner).start()
+            for ring in sorted(set(rings)):
+                members = [o for o, r in zip(offsets, rings) if r == ring]
+                group = ref.at[:, pl.ds(0, len(members)), 0, pl.ds(0, depth)]
+                to(group, group, send, recv.at[ring - 1], partner).wait_recv()
+                for dy, dx in members:
+                    theirs = block(((y + ny - dy) % ny) * nx + (x + nx - dx) % nx)
+                    to(theirs, theirs, turn_send, turn_recv, partner).start()
 
         sent = ref.at[:, pl.ds(0, len(plane)), 0, pl.ds(0, depth)]
         both = ref.at[:, :, 0, pl.ds(0, depth)]
@@ -326,6 +328,7 @@
     ret_o_copy = to(ret_o, face_o, halo_send.at[6], halo_recv.at[6], previous)
     ret_o_copy.start()
     take_back(count - 1)
+    turn()
     halo[4].wait_recv()
     relayed.wait_recv()
     period = min(LANES // 8 * own_rows, span)
@@ -344,7 +347,6 @@
             [mm(shifted[:, k : k + period], chosen) for k in range(0, span, period)], 1
         ).astype(BF16)
 
-    turn()
     turn2()
     c_copies.wait_recv()
 
@@ -478,9 +480,9 @@
             vmem((2 * nz, 1, LANES), F32),
             vmem((ny * nx, 1, LANES), F32),
             dma((7,)), dma((9,)), dma((9,)),
-            dma, dma, dma, dma((ny * nx - 1,)), dma, dma,
+            dma, dma, dma, dma((ny // 2 + nx // 2,)), dma, dma,
             dma, dma, dma, dma,
-            dma, dma, dma, dma((ny * nx - 1,)), dma, dma,
+            dma, dma, dma, dma((ny // 2 + nx // 2,)), dma, dma,
         ]
         projected, image, steps = pl.pallas_call(
             functools.partial(kernel, (nz, ny, nx)),

time: 36.7 us -> 36.6 us (level)
  no operation moved by 1% of the time
where the time goes in v6:
time: 36.6 us; the launch traced here: 36.5 us
  Pallas kernels  34.7 us (95%)
  other arithmetic  1.02 us (3%)
  between operations  0.71 us (2%)
    pallas_call x1, Pallas kernels, on_device(): pl.pallas_call(functools.partial(kernel, (nz, ny, nx)), out_shape=(field,...  34.7 us
    add x1, other arithmetic, on_device(): multipliers + alpha * direction  1.01 us

profile of v6, /device:TPU:1, one launch (start us, length us, event | category | flops | bytes accessed | tf_op | source)
XLA Modules:
  0.0 36.5 jit_solution(18171656879499816139)
XLA Ops:
  0.6 0.0 copy-start.1
  0.6 0.0 copy-start
  0.7 0.0 copy-start.2
  0.7 34.7 %shard_map.103 = (f32[4,32,512]{2,1,0:T(8,128)S(1)}, f32[4,32,512]{2,1,0:T(8,128)S(1)}, f32[2,32,512]{2,1,0:T(8,128)S(1)}) custom-call(f32[4,32,512]{2,1,0:T(8,128)} %res_h.1, f32[4,32,512]{2,1,0:T(8,128)} %old_h.1, s32[4,512]{1,0:T(4,128)} %mat_h.1, bf16[4,1024,1024]{2,1,0:T(8,128)(2,1)} %fac_h.1, f32[6,4,1024]{2,1,0:T(4,128)} %bitcast.8, ...), custom_call_target="tpu_custom_call" | custom-call | tf_op jit(solution)/shard_map/pallas_call | solution.py:487
  35.4 0.0 copy-done.1
  35.4 0.0 copy-done
  35.4 0.0 copy-done.2
  35.5 1.0 %multiply_add_fusion = (f32[4,32,512]{2,1,0:T(8,128)}, f32[4,32,512]{2,1,0:T(8,128)}, f32[4,32,512]{2,1,0:T(8,128)}) fusion(f32[4,32,512]{2,1,0:T(8,128)S(1)} %copy-done.2, f32[32,512]{1,0:T(8,128)S(1)} %get-tuple-element.12, f32[4,32,512]{2,1,0:T(8,128)S(1)} %get-tuple-element.7, f32[4]{0:T(128)S(1)} %compare_convert_fusion, f32[4,32,512]{2,1,0:T(8,128)S(1)} %copy-done.1, ...), kind=kLoop, calls=%fused_computation.1 | loop fusion | flops 524288 | bytes 2228240 | tf_op jit(solution)/shard_map/add | solution.py:501
  (2 shorter events, 0.0 us)
Async XLA Ops:
  0.6 34.8 %copy-start.1 = (f32[4,32,512]{2,1,0:T(8,128)S(1)}, f32[4,32,512]{2,1,0:T(8,128)}, u32[]{:S(2)}) copy-start(f32[4,32,512]{2,1,0:T(8,128)} %old_h.1) | copy-start | bytes 786436
  0.6 34.8 %copy-start = (f32[4,32,512]{2,1,0:T(8,128)S(1)}, f32[4,32,512]{2,1,0:T(8,128)}, u32[]{:S(2)}) copy-start(f32[4,32,512]{2,1,0:T(8,128)} %res_h.1) | copy-start | bytes 786436
  0.7 34.8 %copy-start.2 = (f32[4,32,512]{2,1,0:T(8,128)S(1)}, f32[4,32,512]{2,1,0:T(8,128)}, u32[]{:S(2)}) copy-start(f32[4,32,512]{2,1,0:T(8,128)} %param.8) | copy-start | bytes 786436

commit v7 on v6

--- a/solution.py
+++ b/solution.py
@@ -37,7 +37,7 @@
     resf, oldf, onorm, mat, fac, rigt, rig, rhalo, nr, coa, rows_in, rows_out, relay, cpair, cpair2, table, ubig, lin, m24,
     zb, zb2, gat, gat2, inner_o, inner_m, w_o, face_o, face_p, ret_o, ret_p, arz, arp,
     local_sem, halo_send, halo_recv, z_send, z_recv, y_send, y_recv, c_send, c_recv,
-    az_send, az_recv, ap_send, ap_recv, z2_send, z2_recv, y2_send, y2_recv, c2_send, c2_recv,
+    az_recv, ap_recv, z2_send, z2_recv, y2_send, y2_recv, c2_send, c2_recv,
 ):
     nz, ny, nx = grid
     count, cases, half = p_out.shape
@@ -159,11 +159,14 @@
         to(res_h.at[count - 1], resf.at[0], halo_send.at[0], halo_recv.at[0], following),
         to(nr.at[0], nr.at[count], halo_send.at[1], halo_recv.at[1], previous),
         to(rig.at[count - 1, :, pl.ds(half, half)], rhalo, halo_send.at[2], halo_recv.at[2], following),
-        to(old_h.at[count - 1], oldf.at[0], halo_send.at[3], halo_recv.at[3], following),
-        to(rows_in.at[some], coa.at[edge, some], halo_send.at[4], halo_recv.at[4], partner),
-        to(rows_out.at[some], relay.at[some], halo_send.at[5], halo_recv.at[5], partner),
+        to(old_h.at[count - 1], oldf.at[0], halo_send.at[0], halo_recv.at[0], following),
+        to(rows_in.at[some], coa.at[edge, some], halo_send.at[3], halo_recv.at[3], partner),
+        to(rows_out.at[some], relay.at[some], halo_send.at[3], halo_recv.at[6], partner),
     ]
-    relayed = to(relay.at[some], coa.at[edge, some], halo_send.at[8], halo_recv.at[8], beyond)
+    relayed = to(relay.at[some], coa.at[edge, some], halo_send.at[3], halo_recv.at[3], beyond)
+    two_faces = to(resf.at[pl.ds(0, 2)], resf.at[pl.ds(0, 2)], halo_send.at[0], halo_recv.at[0], partner)
+    two_ends = to(coa.at[pl.ds(0, 2), some], coa.at[pl.ds(0, 2), some], halo_send.at[3], halo_recv.at[3], partner)
+    three_ends = to(coa.at[pl.ds(0, 3), some], coa.at[pl.ds(0, 3), some], halo_send.at[3], halo_recv.at[3], partner)
 
     @pl.when(jnp.logical_not(is_first))
     def _():
@@ -314,9 +317,8 @@
     for zl in range(per_chunk):
         gat2[zl, slot, core, :ranks] = packed(zb2, zl, 0)[:ranks]
     y2_copies, c2_copies, turn2 = to_plane(gat2, ranks, y2_send, y2_recv, c2_send, c2_recv)
-    halo[0].wait_recv()
+    two_faces.wait_recv()
     halo[2].wait_recv()
-    halo[3].wait_recv()
     resf[0] = jnp.where(is_first, 0.0, resf[0])
     place(0, True)
     place(count, False)
@@ -325,12 +327,11 @@
         apply_all(q)
     keep((0, taken), ubig[:, half:], slice(0, count * half))
     take_back(0)
-    ret_o_copy = to(ret_o, face_o, halo_send.at[6], halo_recv.at[6], previous)
+    ret_o_copy = to(ret_o, face_o, halo_send.at[4], halo_recv.at[4], previous)
     ret_o_copy.start()
     take_back(count - 1)
     turn()
-    halo[4].wait_recv()
-    relayed.wait_recv()
+    two_ends.wait_recv()
     period = min(LANES // 8 * own_rows, span)
     kept = period // own_rows * 8
     source = lax.broadcasted_iota(jnp.int32, (period, kept), 0)
@@ -392,7 +393,7 @@
     here = 2 * z + core
     arz[here] = square[0:1] + sum(pltpu.roll(square[i : i + 1], i * cases, 1) for i in range(1, CHUNKS))
     pairs_of = [device for both in zip(line, across) for device in both]
-    az_copies = along_line(arz, here, az_send, az_recv, [*pairs_of, partner])
+    az_copies = along_line(arz, here, z_send, az_recv, [*pairs_of, partner])
 
     for q in range(count):
         solved, returned = backward(inners[q], q)
@@ -401,11 +402,11 @@
             w_out[q - 1] += returned
         else:
             ret_p[...] = returned
-            ret_p_copy = to(ret_p, face_p, halo_send.at[7], halo_recv.at[7], previous)
+            ret_p_copy = to(ret_p, face_p, halo_send.at[5], halo_recv.at[5], previous)
             ret_p_copy.start()
     az_copies.wait()
     arp[slot] = sum(arz[i] for i in range(2 * nz))
-    ap_copies = along_line(arp, slot, ap_send, ap_recv, plane)
+    ap_copies = along_line(arp, slot, z2_send, ap_recv, plane)
     loads[6].wait()
     ret_o_copy.wait()
     ret_p_copy.wait()
@@ -415,7 +416,7 @@
     def _():
         halo[1].wait_send()
 
-    for copy in (halo[0], *halo[2:], relayed, y_copies, c_copies, y2_copies, c2_copies):
+    for copy in (two_faces, halo[2], three_ends, y_copies, c_copies, y2_copies, c2_copies):
         copy.wait_send()
     ap_copies.wait()
     totals = sum(arp[i] for i in range(ny * nx))
@@ -479,9 +480,9 @@
             vmem((cases, half), F32),
             vmem((2 * nz, 1, LANES), F32),
             vmem((ny * nx, 1, LANES), F32),
-            dma((7,)), dma((9,)), dma((9,)),
+            dma((7,)), dma((6,)), dma((7,)),
             dma, dma, dma, dma((ny // 2 + nx // 2,)), dma, dma,
-            dma, dma, dma, dma,
+            dma, dma,
             dma, dma, dma, dma((ny // 2 + nx // 2,)), dma, dma,
         ]
         projected, image, steps = pl.pallas_call(

time: 36.6 us -> 36.5 us (level)
  no operation moved by 1% of the time
where the time goes in v7:
time: 36.5 us; the launch traced here: 36.4 us
  Pallas kernels  34.7 us (95%)
  other arithmetic  1.02 us (3%)
  between operations  0.71 us (2%)
    pallas_call x1, Pallas kernels, on_device(): pl.pallas_call(functools.partial(kernel, (nz, ny, nx)), out_shape=(field,...  34.7 us
    add x1, other arithmetic, on_device(): multipliers + alpha * direction  1.01 us

profile of v7, /device:TPU:1, one launch (start us, length us, event | category | flops | bytes accessed | tf_op | source)
XLA Modules:
  0.0 36.4 jit_solution(15157369451283841335)
XLA Ops:
  0.6 0.0 copy-start.1
  0.6 0.0 copy-start
  0.7 0.0 copy-start.2
  0.7 34.7 %shard_map.103 = (f32[4,32,512]{2,1,0:T(8,128)S(1)}, f32[4,32,512]{2,1,0:T(8,128)S(1)}, f32[2,32,512]{2,1,0:T(8,128)S(1)}) custom-call(f32[4,32,512]{2,1,0:T(8,128)} %res_h.1, f32[4,32,512]{2,1,0:T(8,128)} %old_h.1, s32[4,512]{1,0:T(4,128)} %mat_h.1, bf16[4,1024,1024]{2,1,0:T(8,128)(2,1)} %fac_h.1, f32[6,4,1024]{2,1,0:T(4,128)} %bitcast.8, ...), custom_call_target="tpu_custom_call" | custom-call | tf_op jit(solution)/shard_map/pallas_call | solution.py:488
  35.4 0.0 copy-done.1
  35.4 0.0 copy-done
  35.4 0.0 copy-done.2
  35.4 1.0 %multiply_add_fusion = (f32[4,32,512]{2,1,0:T(8,128)}, f32[4,32,512]{2,1,0:T(8,128)}, f32[4,32,512]{2,1,0:T(8,128)}) fusion(f32[4,32,512]{2,1,0:T(8,128)S(1)} %copy-done.2, f32[32,512]{1,0:T(8,128)S(1)} %get-tuple-element.12, f32[4,32,512]{2,1,0:T(8,128)S(1)} %get-tuple-element.7, f32[4]{0:T(128)S(1)} %compare_convert_fusion, f32[4,32,512]{2,1,0:T(8,128)S(1)} %copy-done.1, ...), kind=kLoop, calls=%fused_computation.1 | loop fusion | flops 524288 | bytes 2228240 | tf_op jit(solution)/shard_map/add | solution.py:502
  (2 shorter events, 0.0 us)
Async XLA Ops:
  0.6 34.7 %copy-start.1 = (f32[4,32,512]{2,1,0:T(8,128)S(1)}, f32[4,32,512]{2,1,0:T(8,128)}, u32[]{:S(2)}) copy-start(f32[4,32,512]{2,1,0:T(8,128)} %old_h.1) | copy-start | bytes 786436
  0.6 34.7 %copy-start = (f32[4,32,512]{2,1,0:T(8,128)S(1)}, f32[4,32,512]{2,1,0:T(8,128)}, u32[]{:S(2)}) copy-start(f32[4,32,512]{2,1,0:T(8,128)} %res_h.1) | copy-start | bytes 786436
  0.7 34.7 %copy-start.2 = (f32[4,32,512]{2,1,0:T(8,128)S(1)}, f32[4,32,512]{2,1,0:T(8,128)}, u32[]{:S(2)}) copy-start(f32[4,32,512]{2,1,0:T(8,128)} %param.8) | copy-start | bytes 786436
